TPU v7x, 32 devices: a whole 2x2x4 slice. The times are simulated.
32 devices in a mesh: district: 16 (over z, y, x), coarse: 2 (over core).
Axes of the slice: x: 2, y: 2, z: 4, core: 2. Of those that a mesh axis runs over, the one named last changes fastest.
Arguments:
- free_response: float32 [128, 16, 512], P(('district', 'coarse')), may hold values from -6 to 6
- flexibility: bfloat16 [128, 512, 512], P(('district', 'coarse')), as said below
- corner_modes: bfloat16 [128, 8, 512], P(('district', 'coarse')), may hold values from -0.5 to 0.5
- corner_owner: int32 [128, 8], P(('district', 'coarse')), may hold values from 0 to 255
- coarse_inverse: float32 [16, 256, 256], P('district'), as said below
- iface_blocks: int32 [128], P(('district', 'coarse')), may hold values from 2 to 4, as said below
- partner: int32 [128, 4], P(('district', 'coarse')), may hold values from -1 to 511, as said below
Outputs:
- multiplier: float32 [128, 16, 512], P(('district', 'coarse'))
- residual: float32 [128, 16, 512], P(('district', 'coarse'))
Inputs may be any that keep to these rules, and one draw needn't show every extreme that they name: `iface_blocks`: every subdomain uses 128 times this many interface unknowns, its first blocks. partner[s, b] is the global block index of the block that shares interface block b of subdomain s; pairs are mutual. Unused blocks, and used blocks against the ground, hold -1. A partner lies on the same coarse index and on the next or previous district index (district closes into a loop). Exactly 4 blocks of each device pair with blocks of the next device along district, and so exactly 4 with the previous one; no block pairs within its own device. `flexibility`: symmetric positive definite, every eigenvalue between 1/2 and 10. `coarse_inverse`: symmetric positive definite, every eigenvalue between 1/2 and 10.
All inputs are finite; a program needn't handle non-finite values.
Results may differ from a plain program's by a relative error of at most 0.007.
Values sent between devices are 32-bit elements; how exact they have to be, the bound alone decides.
No kernel may reach another device: no remote copies, remote signals or barrier semaphores. Data moves between devices by JAX's collectives and lax.ppermute only.
A program may use at most 64 MiB of HBM per device.

v0:
```python
import functools

import jax
import jax.numpy as jnp
from jax import lax
from jax.experimental import pallas as pl
from jax.experimental.pallas import tpu as pltpu
from jax.sharding import PartitionSpec as P


SIDE = 4
AXES = ("district", "coarse")
VMEM = pl.BlockSpec(memory_space=pltpu.VMEM)
HBM = pl.BlockSpec(memory_space=pltpu.MemorySpace.HBM)
F32 = jnp.float32
BF16 = jnp.bfloat16
TILE = 8
LANES = 128


def quotient(value, by):
    if by & (by - 1) == 0:
        return lax.shift_right_logical(value, jnp.int32(by.bit_length() - 1))
    return lax.div(value, jnp.int32(by))


def remainder(value, by):
    if by & (by - 1) == 0:
        return lax.bitwise_and(value, jnp.int32(by - 1))
    return lax.rem(value, jnp.int32(by))


def near_side(index):
    return jnp.where(remainder(index, 2) == 0, index + 1, index - 1)


def far_side(index, count):
    return jnp.where(
        remainder(index, 2) == 0,
        jnp.where(index == 0, count - 1, index - 1),
        jnp.where(index == count - 1, 0, index + 1),
    )


def facing(partner_ref, dims):
    index = lax.axis_index("district")
    near = near_side(index)
    far = far_side(index, dims.districts)
    out = []
    for slot in range(dims.slots):
        for block in range(dims.blocks):
            place = partner_ref[slot, block]
            paired = place >= 0
            safe = jnp.maximum(place, 0)
            district = quotient(safe, dims.coarse * dims.per_device)
            out.append(
                (
                    jnp.logical_and(paired, district == near).astype(jnp.int32),
                    jnp.logical_and(paired, district == far).astype(jnp.int32),
                    remainder(safe, dims.per_device),
                )
            )
    return out


def block_of(ref, slot, block):
    return ref[slot, :, block * LANES : (block + 1) * LANES]


def pack_first_kernel(
    dims, partner_hbm, free_hbm, near_ref, far_ref, free_ref, partner_ref, order, sems
):
    fetch_partner = pltpu.make_async_copy(partner_hbm, partner_ref, sems.at[0])
    fetch_free = pltpu.make_async_copy(free_hbm, free_ref, sems.at[1])
    fetch_partner.start()
    fetch_free.start()
    fetch_partner.wait()
    near_count = jnp.int32(0)
    far_count = jnp.int32(0)
    for place, (near, far, _) in enumerate(facing(partner_ref, dims)):
        slot = jnp.where(near > 0, near_count, jnp.where(far > 0, SIDE + far_count, 2 * SIDE))
        order[slot] = jnp.int32(place)
        near_count += near
        far_count += far
    fetch_free.wait()
    for slot in range(2 * SIDE):
        place = order[slot]
        lane = pl.multiple_of(remainder(place, dims.blocks) * LANES, LANES)
        value = free_ref[quotient(place, dims.blocks), :, pl.ds(lane, LANES)]
        if slot < SIDE:
            near_ref[slot] = value
        else:
            far_ref[slot - SIDE] = value


def prepare_kernel(
    dims,
    partner_hbm,
    iface_hbm,
    owner_hbm,
    modes_hbm,
    inverse_hbm,
    flex_hbm,
    take_ref,
    give_ref,
    weight_ref,
    modes_out,
    onehot_out,
    inverse_out,
    flex_out,
    partner_ref,
    iface_ref,
    owner_ref,
    modes_ref,
    inverse_ref,
    partners,
    sems,
):
    pairs = (
        (partner_hbm, partner_ref),
        (iface_hbm, iface_ref),
        (owner_hbm, owner_ref),
        (modes_hbm, modes_ref),
        (inverse_hbm, inverse_ref),
        (flex_hbm, flex_out),
    )
    fetches = [
        pltpu.make_async_copy(there, here, sems.at[i]) for i, (there, here) in enumerate(pairs)
    ]
    for fetch in fetches:
        fetch.start()
    for fetch in fetches[:-1]:
        fetch.wait()
    faces = facing(partner_ref, dims)
    row = lax.broadcasted_iota(jnp.int32, (TILE, LANES), 0)
    near_count = jnp.int32(0)
    far_count = jnp.int32(0)
    for place, (near, far, other) in enumerate(faces):
        slot = jnp.where(near > 0, near_count, jnp.where(far > 0, SIDE + far_count, 2 * SIDE))
        partners[slot] = other
        give_ref[place] = jnp.where(row == slot, 1.0, 0.0).astype(F32)
        near_count += near
        far_count += far
    for place, (near, far, other) in enumerate(faces):
        slot_id, block_id = divmod(place, dims.blocks)
        from_near = jnp.int32(0)
        from_far = jnp.int32(SIDE)
        for slot in range(SIDE):
            from_near += (partners[slot] < other).astype(jnp.int32)
            from_far += (partners[SIDE + slot] < other).astype(jnp.int32)
        slot = jnp.where(near > 0, from_near, jnp.where(far > 0, from_far, 2 * SIDE))
        take_ref[place] = jnp.where(row == slot, 1.0, 0.0).astype(F32)
        used = (block_id < iface_ref[slot_id]).astype(F32)
        double = used + jnp.maximum(near, far).astype(F32)
        weight_ref[place] = jnp.where(row == 0, used, double)
    corner_rows = dims.slots * dims.corners
    slot_of_row = quotient(
        lax.broadcasted_iota(jnp.int32, (corner_rows, dims.width), 0), dims.corners
    )
    for slot in range(dims.slots):
        modes = modes_ref[slot].astype(F32)
        stacked = jnp.concatenate([modes] * dims.slots, axis=0)
        modes_out[:, slot * dims.width : (slot + 1) * dims.width] = jnp.where(
            slot_of_row == slot, stacked, 0.0
        ).astype(BF16)
    corner = lax.broadcasted_iota(jnp.int32, (dims.corners, dims.coarse_width), 0)
    column = lax.broadcasted_iota(jnp.int32, (dims.corners, dims.coarse_width), 1)
    hot = []
    for slot in range(dims.slots):
        owners = jnp.zeros((dims.corners, dims.coarse_width), jnp.int32)
        for k in range(dims.corners):
            owners = jnp.where(corner == k, owner_ref[slot, k], owners)
        hot.append(jnp.where(column == owners, 1.0, 0.0).astype(F32))
    onehot = jnp.concatenate(hot, axis=0)
    onehot_out[...] = onehot.astype(BF16)
    inverse_out[...] = lax.dot_general(
        inverse_ref[0],
        onehot,
        (((1,), (1,)), ((), ())),
        precision=lax.Precision.HIGHEST,
        preferred_element_type=F32,
    )
    fetches[-1].wait()


def halves(value):
    high = value.astype(BF16)
    low = (value - high.astype(F32)).astype(BF16)
    return high, low


def lane_sums(value):
    return jnp.sum(value, axis=0, keepdims=True)


def jump_blocks(dims, field_ref, near_ref, far_ref, take_ref, weight_ref):
    for slot in range(dims.slots):
        for block in range(dims.blocks):
            place = slot * dims.blocks + block
            value = block_of(field_ref, slot, block) * weight_ref[place, 0:1, :]
            for side, ref in enumerate((near_ref, far_ref)):
                for j in range(SIDE):
                    row = side * SIDE + j
                    value = value - take_ref[place, row : row + 1, :] * ref[j]
            yield slot, block, value


def coarse_part(dims, high_parts, low_parts, modes_ref, onehot_ref):
    rows = dims.scen
    stacked = jnp.concatenate(
        [jnp.concatenate(high_parts, axis=1), jnp.concatenate(low_parts, axis=1)], axis=0
    )
    sums = lax.dot_general(
        stacked, modes_ref[...], (((1,), (1,)), ((), ())), preferred_element_type=F32
    )
    sums = sums[:rows] + sums[rows:]
    first, rest = halves(sums)
    rest = sums - first.astype(F32)
    second, third = halves(rest)
    pieces = jnp.dot(
        jnp.concatenate([first, second, third], axis=0),
        onehot_ref[...],
        preferred_element_type=F32,
    )
    return pieces[:rows] + pieces[rows : 2 * rows] + pieces[2 * rows :]


def jump_kernel(
    dims,
    field_ref,
    near_ref,
    far_ref,
    take_ref,
    weight_ref,
    modes_ref,
    onehot_ref,
    jump_ref,
    coarse_ref,
):
    high_parts, low_parts = [], []
    for slot, block, value in jump_blocks(
        dims, field_ref, near_ref, far_ref, take_ref, weight_ref
    ):
        jump_ref[slot, :, block * LANES : (block + 1) * LANES] = value
        high, low = halves(value)
        high_parts.append(high)
        low_parts.append(low)
    coarse_ref[...] = coarse_part(dims, high_parts, low_parts, modes_ref, onehot_ref)


def local_kernel(dims, direction_ref, flex_ref, out_ref):
    for slot in range(dims.slots):
        high, low = halves(direction_ref[slot])
        both = jnp.dot(
            jnp.concatenate([high, low], axis=0), flex_ref[slot], preferred_element_type=F32
        )
        out_ref[slot] = both[: dims.scen] + both[dims.scen :]


def local_last_kernel(dims, direction_ref, flex_ref, rhs_ref, out_ref, sums_ref):
    local_kernel(dims, direction_ref, flex_ref, out_ref)
    acc = [jnp.zeros((dims.scen, LANES), F32)] * 3
    for slot in range(dims.slots):
        for block in range(dims.blocks):
            rhs = block_of(rhs_ref, slot, block)
            image = block_of(direction_ref, slot, block)
            acc[0] = acc[0] + rhs * rhs
            acc[1] = acc[1] + rhs * image
            acc[2] = acc[2] + image * image
    sums_ref[...] = rows_of(acc, 0)


def rows_of(parts, first):
    row = lax.broadcasted_iota(jnp.int32, (TILE, LANES), 0)
    tile = jnp.zeros((TILE, LANES), F32)
    for q, part in enumerate(parts):
        tile = jnp.where(row == first + q, lane_sums(part), tile)
    return tile


def add_coarse(dims, local_ref, total, modes_ref, inverse_ref):
    values = jnp.dot(
        total, inverse_ref[...], precision=lax.Precision.HIGHEST, preferred_element_type=F32
    )
    high, low = halves(values)
    both = jnp.dot(
        jnp.concatenate([high, low], axis=0), modes_ref[...], preferred_element_type=F32
    )
    both = both[: dims.scen] + both[dims.scen :]
    return [
        local_ref[slot] + both[:, slot * dims.width : (slot + 1) * dims.width]
        for slot in range(dims.slots)
    ]


def pack(dims, response, give_ref, near_ref, far_ref):
    for side, ref in enumerate((near_ref, far_ref)):
        for j in range(SIDE):
            row = side * SIDE + j
            value = jnp.zeros((dims.scen, LANES), F32)
            for place in range(dims.per_device):
                slot, block = divmod(place, dims.blocks)
                part = response[slot][:, block * LANES : (block + 1) * LANES]
                value = value + give_ref[place, row : row + 1, :] * part
            ref[j] = value


def respond_kernel(
    dims,
    local_ref,
    own_ref,
    other_ref,
    modes_ref,
    inverse_ref,
    give_ref,
    out_ref,
    near_ref,
    far_ref,
):
    response = add_coarse(dims, local_ref, own_ref[...] + other_ref[...], modes_ref, inverse_ref)
    for slot in range(dims.slots):
        out_ref[slot] = response[slot]
    pack(dims, response, give_ref, near_ref, far_ref)


def respond_last_kernel(
    dims,
    local_ref,
    own_ref,
    other_ref,
    modes_ref,
    inverse_ref,
    give_ref,
    weight_ref,
    rhs_ref,
    image_ref,
    early_ref,
    out_ref,
    near_ref,
    far_ref,
    sums_ref,
):
    response = add_coarse(dims, local_ref, own_ref[...] + other_ref[...], modes_ref, inverse_ref)
    acc = [jnp.zeros((dims.scen, LANES), F32)] * 2
    for slot in range(dims.slots):
        out_ref[slot] = response[slot]
        for block in range(dims.blocks):
            place = slot * dims.blocks + block
            doubled = weight_ref[place, 1:2, :] * response[slot][
                :, block * LANES : (block + 1) * LANES
            ]
            acc[0] = acc[0] + block_of(rhs_ref, slot, block) * doubled
            acc[1] = acc[1] + block_of(image_ref, slot, block) * doubled
    sums_ref[...] = jnp.broadcast_to((early_ref[...] + rows_of(acc, 3))[None], sums_ref.shape)
    pack(dims, response, give_ref, near_ref, far_ref)


def finish_kernel(
    dims,
    sums_ref,
    rhs_ref,
    image_ref,
    field_ref,
    near_ref,
    far_ref,
    take_ref,
    weight_ref,
    multiplier_ref,
    residual_ref,
):
    totals = jnp.sum(jnp.sum(sums_ref[...], axis=0), axis=1, keepdims=True)
    norm, first, square, cross, second = (totals[q : q + 1, :] for q in range(5))
    step = norm / first
    norm_next = norm - 2.0 * step * first + step * step * square
    grown = 1.0 + norm_next / norm
    curve = grown * grown * first - grown * step * (cross + square) + step * step * second
    step_next = norm_next / curve
    on_first = step + step_next * grown
    on_second = step_next * step
    for slot, block, second_image in jump_blocks(
        dims, field_ref, near_ref, far_ref, take_ref, weight_ref
    ):
        lanes = slice(block * LANES, (block + 1) * LANES)
        rhs = rhs_ref[slot, :, lanes]
        image = image_ref[slot, :, lanes]
        multiplier_ref[slot, :, lanes] = on_first * rhs - on_second * image
        residual_ref[slot, :, lanes] = rhs - on_first * image + on_second * second_image


class Dims:
    pass


def stay(value):
    return pltpu.with_memory_space_constraint(value, pltpu.MemorySpace.HBM)


def call(kernel, dims, outs, args, in_specs=None, out_specs=None, scratch=(), cost=None):
    return pl.pallas_call(
        functools.partial(kernel, dims),
        out_shape=outs,
        in_specs=in_specs if in_specs is not None else [VMEM] * len(args),
        out_specs=out_specs if out_specs is not None else jax.tree.map(lambda _: VMEM, outs),
        scratch_shapes=list(scratch),
        compiler_params=pltpu.CompilerParams(vmem_limit_bytes=16 << 20),
        cost_estimate=cost,
    )(*args)


def local(
    free_response, flexibility, corner_modes, corner_owner, coarse_inverse, iface_blocks, partner
):
    dims = Dims()
    dims.slots, dims.scen, dims.width = free_response.shape
    dims.blocks = partner.shape[1]
    dims.per_device = dims.slots * dims.blocks
    dims.coarse_width = coarse_inverse.shape[1]
    dims.corners = corner_modes.shape[1]
    dims.districts = lax.axis_size("district")
    dims.coarse = lax.axis_size("coarse")
    devices = dims.districts * dims.coarse
    shape = jax.ShapeDtypeStruct
    whole = shape(free_response.shape, F32)
    packed = shape((SIDE, dims.scen, LANES), F32)
    per_block = shape((dims.per_device, TILE, LANES), F32)
    corner_rows = dims.slots * dims.corners

    near_pairs = [(d, d + 1 if d % 2 == 0 else d - 1) for d in range(dims.districts)]
    far_pairs = [
        (d, (d - 1 if d % 2 == 0 else d + 1) % dims.districts) for d in range(dims.districts)
    ]

    def exchange(near, far):
        far = lax.ppermute(far, "district", far_pairs)
        near = lax.ppermute(near, "district", near_pairs)
        return near, far

    def from_group(value):
        if dims.coarse == 2:
            return lax.ppermute(value, "coarse", [(0, 1), (1, 0)])
        return lax.psum(value, "coarse") - value

    near, far, field = call(
        pack_first_kernel,
        dims,
        (packed, packed, whole),
        (stay(partner), stay(free_response)),
        in_specs=[HBM, HBM],
        scratch=[
            pltpu.SMEM(partner.shape, jnp.int32),
            pltpu.SMEM((2 * SIDE + 1,), jnp.int32),
            pltpu.SemaphoreType.DMA((2,)),
        ],
    )
    near, far = exchange(near, far)
    take, give, weight, modes, onehot, inverse, flex = call(
        prepare_kernel,
        dims,
        (
            per_block,
            per_block,
            per_block,
            shape((corner_rows, dims.slots * dims.width), BF16),
            shape((corner_rows, dims.coarse_width), BF16),
            shape((dims.coarse_width, corner_rows), F32),
            shape(flexibility.shape, BF16),
        ),
        tuple(
            stay(value)
            for value in (
                partner,
                iface_blocks,
                corner_owner,
                corner_modes,
                coarse_inverse,
                flexibility,
            )
        ),
        in_specs=[HBM] * 6,
        scratch=[
            pltpu.SMEM(partner.shape, jnp.int32),
            pltpu.SMEM(iface_blocks.shape, jnp.int32),
            pltpu.SMEM(corner_owner.shape, jnp.int32),
            pltpu.VMEM(corner_modes.shape, BF16),
            pltpu.VMEM(coarse_inverse.shape, F32),
            pltpu.SMEM((2 * SIDE + 1,), jnp.int32),
            pltpu.SemaphoreType.DMA((6,)),
        ],
        cost=pl.CostEstimate(flops=10**7, bytes_accessed=4 * 10**6, transcendentals=0),
    )

    def jump(field, near, far):
        return call(
            jump_kernel,
            dims,
            (whole, shape((dims.scen, dims.coarse_width), F32)),
            (field, near, far, take, weight, modes, onehot),
        )

    matmul_cost = pl.CostEstimate(flops=10**8, bytes_accessed=3 * 10**6, transcendentals=0)
    rhs, part = jump(field, near, far)
    other = from_group(part)
    term = call(local_kernel, dims, whole, (rhs, flex), cost=matmul_cost)
    response, near, far = call(
        respond_kernel,
        dims,
        (whole, packed, packed),
        (term, part, other, modes, inverse, give),
    )
    near, far = exchange(near, far)
    image, part = jump(response, near, far)
    other = from_group(part)
    term, early = call(
        local_last_kernel,
        dims,
        (whole, shape((TILE, LANES), F32)),
        (image, flex, rhs),
        cost=matmul_cost,
    )
    response, near, far, sums = call(
        respond_last_kernel,
        dims,
        (whole, packed, packed, shape((devices, TILE, LANES), F32)),
        (term, part, other, modes, inverse, give, weight, rhs, image, early),
    )
    sums = lax.all_to_all(sums, AXES, 0, 0)
    near, far = exchange(near, far)
    return call(
        finish_kernel,
        dims,
        (whole, whole),
        (sums, rhs, image, response, near, far, take, weight),
    )


def solution(mesh):
    in_specs = (
        P(AXES, None, None),
        P(AXES, None, None),
        P(AXES, None, None),
        P(AXES, None),
        P("district", None, None),
        P(AXES),
        P(AXES, None),
    )
    out_specs = (P(AXES, None, None), P(AXES, None, None))
    return jax.shard_map(local, mesh=mesh, in_specs=in_specs, out_specs=out_specs, check_vma=False)
```

profile of v0, /device:TPU:0, one launch (start us, length us, event | category | flops | bytes accessed | tf_op | source)
XLA Modules:
  0.0 39.5 jit_solution(17921017853372817279)
XLA Ops:
  0.6 0.9 %shard_map.86 = (f32[4,16,128]{2,1,0:T(8,128)S(1)}, f32[4,16,128]{2,1,0:T(8,128)S(1)}, f32[4,16,512]{2,1,0:T(8,128)S(1)}) custom-call(s32[4,4]{1,0:T(4,128)} %partner_hbm.3, f32[4,16,512]{2,1,0:T(8,128)} %free_hbm.1), custom_call_target="tpu_custom_call" | custom-call | tf_op jit(solution)/shard_map/pallas_call | solution.py:399
  1.6 3.0 %collective-permute-start = (f32[4,16,128]{2,1,0:T(8,128)S(1)}, f32[4,16,128]{2,1,0:T(8,128)S(1)}, u32[]{:S(2)}, u32[]{:S(2)}) collective-permute-start(f32[4,16,128]{2,1,0:T(8,128)S(1)} %get-tuple-element.26), channel_id=1, source_target_pairs={{0,2},{2,0},{4,6},{6,4},{8,10},{10,8},{12,14},{14,12},{16,18},{18,... | collective-permute-start | bytes 98312 | tf_op jit(solution)/shard_map/ppermute | solution.py:435
  4.6 4.5 %collective-permute-start.1 = (f32[4,16,128]{2,1,0:T(8,128)S(1)}, f32[4,16,128]{2,1,0:T(8,128)S(1)}, u32[]{:S(2)}, u32[]{:S(2)}) collective-permute-start(f32[4,16,128]{2,1,0:T(8,128)S(1)} %get-tuple-element.27), channel_id=1, source_target_pairs={{0,30},{2,4},{4,2},{6,8},{8,6},{10,12},{12,10},{14,16},{16,14},{18... | collective-permute-start | bytes 98312 | tf_op jit(solution)/shard_map/ppermute | solution.py:434
  9.1 1.8 %shard_map.87 = (f32[16,8,128]{2,1,0:T(8,128)S(1)}, f32[16,8,128]{2,1,0:T(8,128)S(1)}, f32[16,8,128]{2,1,0:T(8,128)S(1)}, bf16[32,2048]{1,0:T(8,128)(2,1)S(1)}, ...) custom-call(s32[4,4]{1,0:T(4,128)} %partner_hbm.3, s32[4]{0:T(128)} %iface_hbm.1, ...), custom_call_target="tpu_custom_call" | custom-call | flops 10000000 | bytes 4000000 | tf_op jit(solution)/shard_map/pallas_call | solution.py:399
  10.9 0.0 collective-permute-done.near_ref
  10.9 1.2 %collective-permute-done.1.far_ref = f32[4,16,128]{2,1,0:T(8,128)S(1)} collective-permute-done((f32[4,16,128]{2,1,0:T(8,128)S(1)}, f32[4,16,128]{2,1,0:T(8,128)S(1)}, u32[]{:S(2)}, u32[]{:S(2)}) %collective-permute-start.1) | collective-permute-done | bytes 32800 | tf_op jit(solution)/shard_map/ppermute | solution.py:434
  12.1 0.3 shard_map.88
  12.4 0.0 collective-permute-start.2
  12.4 0.5 %shard_map.89.local_ref = f32[4,16,512]{2,1,0:T(8,128)S(1)} custom-call(f32[4,16,512]{2,1,0:T(8,128)S(1)} %get-tuple-element.32.direction_ref.rhs_ref, bf16[4,512,512]{2,1,0:T(8,128)(2,1)S(1)} %get-tuple-element.33.flex_ref), custom_call_target="tpu_custom_call" | custom-call | flops 100000000 | bytes 3000000 | tf_op jit(solution)/shard_map/pallas_call | solution.py:399
  12.9 0.7 %collective-permute-done.2.other_ref = f32[16,256]{1,0:T(8,128)S(1)} collective-permute-done((f32[16,256]{1,0:T(8,128)S(1)}, f32[16,256]{1,0:T(8,128)S(1)}, u32[]{:S(2)}, u32[]{:S(2)}) %collective-permute-start.2) | collective-permute-done | bytes 16416 | tf_op jit(solution)/shard_map/ppermute | solution.py:440
  13.7 0.4 shard_map.90
  14.1 0.1 collective-permute-start.3
  14.1 4.6 %collective-permute-start.4 = (f32[4,16,128]{2,1,0:T(8,128)S(1)}, f32[4,16,128]{2,1,0:T(8,128)S(1)}, u32[]{:S(2)}, u32[]{:S(2)}) collective-permute-start(f32[4,16,128]{2,1,0:T(8,128)S(1)} %get-tuple-element.39), channel_id=1, source_target_pairs={{0,30},{2,4},{4,2},{6,8},{8,6},{10,12},{12,10},{14,16},{16,14},{18... | collective-permute-start | bytes 98312 | tf_op jit(solution)/shard_map/ppermute | solution.py:434
  18.7 0.0 collective-permute-done.3.near_ref
  18.7 3.0 %collective-permute-done.4.far_ref = f32[4,16,128]{2,1,0:T(8,128)S(1)} collective-permute-done((f32[4,16,128]{2,1,0:T(8,128)S(1)}, f32[4,16,128]{2,1,0:T(8,128)S(1)}, u32[]{:S(2)}, u32[]{:S(2)}) %collective-permute-start.4) | collective-permute-done | bytes 32800 | tf_op jit(solution)/shard_map/ppermute | solution.py:434
  21.7 0.3 shard_map.91
  22.0 0.0 collective-permute-start.5
  22.0 0.5 %shard_map.92 = (f32[4,16,512]{2,1,0:T(8,128)S(1)}, f32[8,128]{1,0:T(8,128)S(1)}) custom-call(f32[4,16,512]{2,1,0:T(8,128)S(1)} %get-tuple-element.40.direction_ref.image_ref, bf16[4,512,512]{2,1,0:T(8,128)(2,1)S(1)} %get-tuple-element.33.flex_ref, f32[4,16,512]{2,1,0:T(8,128)S(1)} %get-tuple-element.32.direction_ref.rhs_ref), custom_call_target="tpu_custom_call" | custom-call | flops 100000000 | bytes 3000000 | tf_op jit(solution)/shard_map/pallas_call | solution.py:399
  22.5 0.7 %collective-permute-done.5.other_ref = f32[16,256]{1,0:T(8,128)S(1)} collective-permute-done((f32[16,256]{1,0:T(8,128)S(1)}, f32[16,256]{1,0:T(8,128)S(1)}, u32[]{:S(2)}, u32[]{:S(2)}) %collective-permute-start.5) | collective-permute-done | bytes 16416 | tf_op jit(solution)/shard_map/ppermute | solution.py:440
  23.3 1.1 %shard_map.93 = (f32[4,16,512]{2,1,0:T(8,128)S(1)}, f32[4,16,128]{2,1,0:T(8,128)S(1)}, f32[4,16,128]{2,1,0:T(8,128)S(1)}, f32[32,8,128]{2,1,0:T(8,128)}) custom-call(f32[4,16,512]{2,1,0:T(8,128)S(1)} %get-tuple-element.41.local_ref, f32[16,256]{1,0:T(8,128)S(1)} %get-tuple-element.42.own_ref, f32[16,256]{1,0:T(8,128)S(1)} %collective-permute-done.5.other_ref, ...), custom_call_target="tpu_custom_call" | custom-call | tf_op jit(solution)/shard_map/pallas_call | solution.py:399
  24.3 4.9 %all-to-all-start = ((f32[32,8,128]{2,1,0:T(8,128)}), f32[32,8,128]{2,1,0:T(8,128)S(1)}, u32[]{:S(2)}, u32[]{:S(2)}) async-start(f32[32,8,128]{2,1,0:T(8,128)} %get-tuple-element.44), calls=%async_computation | async-start | bytes 262144 | tf_op jit(solution)/shard_map/all_to_all | solution.py:526
  29.2 1.8 %collective-permute-start.6 = (f32[4,16,128]{2,1,0:T(8,128)S(1)}, f32[4,16,128]{2,1,0:T(8,128)S(1)}, u32[]{:S(2)}, u32[]{:S(2)}) collective-permute-start(f32[4,16,128]{2,1,0:T(8,128)S(1)} %get-tuple-element.46), channel_id=1, source_target_pairs={{0,2},{2,0},{4,6},{6,4},{8,10},{10,8},{12,14},{14,12},{16,18},{18,... | collective-permute-start | bytes 98312 | tf_op jit(solution)/shard_map/ppermute | solution.py:435
  31.1 4.2 %collective-permute-start.7 = (f32[4,16,128]{2,1,0:T(8,128)S(1)}, f32[4,16,128]{2,1,0:T(8,128)S(1)}, u32[]{:S(2)}, u32[]{:S(2)}) collective-permute-start(f32[4,16,128]{2,1,0:T(8,128)S(1)} %get-tuple-element.47), channel_id=1, source_target_pairs={{0,30},{2,4},{4,2},{6,8},{8,6},{10,12},{12,10},{14,16},{16,14},{18... | collective-permute-start | bytes 98312 | tf_op jit(solution)/shard_map/ppermute | solution.py:434
  35.3 0.0 collective-permute-done.6.near_ref
  35.3 3.3 %collective-permute-done.7.far_ref = f32[4,16,128]{2,1,0:T(8,128)S(1)} collective-permute-done((f32[4,16,128]{2,1,0:T(8,128)S(1)}, f32[4,16,128]{2,1,0:T(8,128)S(1)}, u32[]{:S(2)}, u32[]{:S(2)}) %collective-permute-start.7) | collective-permute-done | bytes 32800 | tf_op jit(solution)/shard_map/ppermute | solution.py:434
  38.6 0.0 all-to-all-done.sums_ref
  38.6 0.9 %shard_map.94 = (f32[4,16,512]{2,1,0:T(8,128)}, f32[4,16,512]{2,1,0:T(8,128)}) custom-call(f32[32,8,128]{2,1,0:T(8,128)S(1)} %all-to-all-done.sums_ref, f32[4,16,512]{2,1,0:T(8,128)S(1)} %get-tuple-element.32.direction_ref.rhs_ref, f32[4,16,512]{2,1,0:T(8,128)S(1)} %get-tuple-element.40.direction_ref.image_ref, ...), custom_call_target="tpu_custom_call" | custom-call | tf_op jit(solution)/shard_map/pallas_call | solution.py:399
Async XLA Ops:
  1.6 9.3 %collective-permute-start = (f32[4,16,128]{2,1,0:T(8,128)S(1)}, f32[4,16,128]{2,1,0:T(8,128)S(1)}, u32[]{:S(2)}, u32[]{:S(2)}) collective-permute-start(f32[4,16,128]{2,1,0:T(8,128)S(1)} %get-tuple-element.26), channel_id=1, source_target_pairs={{0,2},{2,0},{4,6},{6,4},{8,10},{10,8},{12,14},{14,12},{16,18},{18,... | collective-permute-start | bytes 98312 | tf_op jit(solution)/shard_map/ppermute | solution.py:435
  4.6 7.5 %collective-permute-start.1 = (f32[4,16,128]{2,1,0:T(8,128)S(1)}, f32[4,16,128]{2,1,0:T(8,128)S(1)}, u32[]{:S(2)}, u32[]{:S(2)}) collective-permute-start(f32[4,16,128]{2,1,0:T(8,128)S(1)} %get-tuple-element.27), channel_id=1, source_target_pairs={{0,30},{2,4},{4,2},{6,8},{8,6},{10,12},{12,10},{14,16},{16,14},{18... | collective-permute-start | bytes 98312 | tf_op jit(solution)/shard_map/ppermute | solution.py:434
  12.4 1.2 %collective-permute-start.2 = (f32[16,256]{1,0:T(8,128)S(1)}, f32[16,256]{1,0:T(8,128)S(1)}, u32[]{:S(2)}, u32[]{:S(2)}) collective-permute-start(f32[16,256]{1,0:T(8,128)S(1)} %get-tuple-element.34.own_ref), channel_id=1, source_target_pairs={{0,1},{1,0},{2,3},{3,2},{4,5},{5,4},{6,7},{7,6},{8,9},{9,8},{10,11... | collective-permute-start | bytes 49160 | tf_op jit(solution)/shard_map/ppermute | solution.py:440
  14.1 4.7 %collective-permute-start.3 = (f32[4,16,128]{2,1,0:T(8,128)S(1)}, f32[4,16,128]{2,1,0:T(8,128)S(1)}, u32[]{:S(2)}, u32[]{:S(2)}) collective-permute-start(f32[4,16,128]{2,1,0:T(8,128)S(1)} %get-tuple-element.38), channel_id=1, source_target_pairs={{0,2},{2,0},{4,6},{6,4},{8,10},{10,8},{12,14},{14,12},{16,18},{18,... | collective-permute-start | bytes 98312 | tf_op jit(solution)/shard_map/ppermute | solution.py:435
  14.1 7.6 %collective-permute-start.4 = (f32[4,16,128]{2,1,0:T(8,128)S(1)}, f32[4,16,128]{2,1,0:T(8,128)S(1)}, u32[]{:S(2)}, u32[]{:S(2)}) collective-permute-start(f32[4,16,128]{2,1,0:T(8,128)S(1)} %get-tuple-element.39), channel_id=1, source_target_pairs={{0,30},{2,4},{4,2},{6,8},{8,6},{10,12},{12,10},{14,16},{16,14},{18... | collective-permute-start | bytes 98312 | tf_op jit(solution)/shard_map/ppermute | solution.py:434
  22.0 1.2 %collective-permute-start.5 = (f32[16,256]{1,0:T(8,128)S(1)}, f32[16,256]{1,0:T(8,128)S(1)}, u32[]{:S(2)}, u32[]{:S(2)}) collective-permute-start(f32[16,256]{1,0:T(8,128)S(1)} %get-tuple-element.42.own_ref), channel_id=1, source_target_pairs={{0,1},{1,0},{2,3},{3,2},{4,5},{5,4},{6,7},{7,6},{8,9},{9,8},{10,11... | collective-permute-start | bytes 49160 | tf_op jit(solution)/shard_map/ppermute | solution.py:440
  24.3 14.2 %all-to-all-start = ((f32[32,8,128]{2,1,0:T(8,128)}), f32[32,8,128]{2,1,0:T(8,128)S(1)}, u32[]{:S(2)}, u32[]{:S(2)}) async-start(f32[32,8,128]{2,1,0:T(8,128)} %get-tuple-element.44), calls=%async_computation | async-start | bytes 262144 | tf_op jit(solution)/shard_map/all_to_all | solution.py:526
  29.2 6.1 %collective-permute-start.6 = (f32[4,16,128]{2,1,0:T(8,128)S(1)}, f32[4,16,128]{2,1,0:T(8,128)S(1)}, u32[]{:S(2)}, u32[]{:S(2)}) collective-permute-start(f32[4,16,128]{2,1,0:T(8,128)S(1)} %get-tuple-element.46), channel_id=1, source_target_pairs={{0,2},{2,0},{4,6},{6,4},{8,10},{10,8},{12,14},{14,12},{16,18},{18,... | collective-permute-start | bytes 98312 | tf_op jit(solution)/shard_map/ppermute | solution.py:435
  31.1 7.5 %collective-permute-start.7 = (f32[4,16,128]{2,1,0:T(8,128)S(1)}, f32[4,16,128]{2,1,0:T(8,128)S(1)}, u32[]{:S(2)}, u32[]{:S(2)}) collective-permute-start(f32[4,16,128]{2,1,0:T(8,128)S(1)} %get-tuple-element.47), channel_id=1, source_target_pairs={{0,30},{2,4},{4,2},{6,8},{8,6},{10,12},{12,10},{14,16},{16,14},{18... | collective-permute-start | bytes 98312 | tf_op jit(solution)/shard_map/ppermute | solution.py:434
where the time goes:
time: 39.7 us; the launch traced here: 39.5 us
  starting transfers between devices  23.2 us (58%)
  waiting for transfers between devices  8.91 us (22%)
  Pallas kernels  6.69 us (17%)
  between operations  0.69 us (2%)
    ppermute x3, starting transfers between devices, exchange(): far = lax.ppermute(far, 'district', far_pairs)  13.4 us
    ppermute x3, waiting for transfers between devices, exchange(): far = lax.ppermute(far, 'district', far_pairs)  7.44 us
    pallas_call x9, Pallas kernels, call(): pl.pallas_call(functools.partial(kernel, dims), out_shape=outs, in_specs=...  6.69 us
    ppermute x3, starting transfers between devices, exchange(): near = lax.ppermute(near, 'district', near_pairs)  4.94 us
    all_to_all x1, starting transfers between devices, local(): sums = lax.all_to_all(sums, AXES, 0, 0)  4.89 us
    ppermute x2, waiting for transfers between devices, from_group(): return lax.ppermute(value, 'coarse', [(0, 1), (1, 0)])  1.46 us
  transfers between devices with their start and end apart: 9, of which 5 were waited for; matrix products, arithmetic and copies ran while one was open for 0% of the time, Pallas kernels for 7%

commit v1 on v0

--- a/solution.py
+++ b/solution.py
@@ -71,9 +71,13 @@
     dims, partner_hbm, free_hbm, near_ref, far_ref, free_ref, partner_ref, order, sems
 ):
     fetch_partner = pltpu.make_async_copy(partner_hbm, partner_ref, sems.at[0])
-    fetch_free = pltpu.make_async_copy(free_hbm, free_ref, sems.at[1])
+    fetch_free = [
+        pltpu.make_async_copy(free_hbm.at[slot], free_ref.at[slot], sems.at[1 + slot])
+        for slot in range(dims.slots)
+    ]
     fetch_partner.start()
-    fetch_free.start()
+    for fetch in fetch_free:
+        fetch.start()
     fetch_partner.wait()
     near_count = jnp.int32(0)
     far_count = jnp.int32(0)
@@ -82,7 +86,8 @@
         order[slot] = jnp.int32(place)
         near_count += near
         far_count += far
-    fetch_free.wait()
+    for fetch in fetch_free:
+        fetch.wait()
     for slot in range(2 * SIDE):
         place = order[slot]
         lane = pl.multiple_of(remainder(place, dims.blocks) * LANES, LANES)
@@ -101,18 +106,20 @@
     modes_hbm,
     inverse_hbm,
     flex_hbm,
+    others_in,
     take_ref,
     give_ref,
     weight_ref,
     modes_out,
-    onehot_out,
-    inverse_out,
+    high_out,
+    low_out,
     flex_out,
     partner_ref,
     iface_ref,
     owner_ref,
     modes_ref,
     inverse_ref,
+    others_ref,
     partners,
     sems,
 ):
@@ -120,6 +127,7 @@
         (partner_hbm, partner_ref),
         (iface_hbm, iface_ref),
         (owner_hbm, owner_ref),
+        (others_in, others_ref),
         (modes_hbm, modes_ref),
         (inverse_hbm, inverse_ref),
         (flex_hbm, flex_out),
@@ -153,33 +161,58 @@
         used = (block_id < iface_ref[slot_id]).astype(F32)
         double = used + jnp.maximum(near, far).astype(F32)
         weight_ref[place] = jnp.where(row == 0, used, double)
-    corner_rows = dims.slots * dims.corners
+    member = lax.axis_index("coarse")
+    all_slots = dims.slots * dims.coarse
+    corner_rows = all_slots * dims.corners
     slot_of_row = quotient(
         lax.broadcasted_iota(jnp.int32, (corner_rows, dims.width), 0), dims.corners
     )
+    placed = []
     for slot in range(dims.slots):
         modes = modes_ref[slot].astype(F32)
-        stacked = jnp.concatenate([modes] * dims.slots, axis=0)
-        modes_out[:, slot * dims.width : (slot + 1) * dims.width] = jnp.where(
-            slot_of_row == slot, stacked, 0.0
-        ).astype(BF16)
+        stacked = jnp.concatenate([modes] * all_slots, axis=0)
+        block = jnp.where(slot_of_row == member * dims.slots + slot, stacked, 0.0).astype(BF16)
+        modes_out[:, slot * dims.width : (slot + 1) * dims.width] = block
+        placed.append(block)
     corner = lax.broadcasted_iota(jnp.int32, (dims.corners, dims.coarse_width), 0)
     column = lax.broadcasted_iota(jnp.int32, (dims.corners, dims.coarse_width), 1)
-    hot = []
-    for slot in range(dims.slots):
+    hot, own_hot = [], []
+    for place in range(all_slots):
+        who, slot = divmod(place, dims.slots)
         owners = jnp.zeros((dims.corners, dims.coarse_width), jnp.int32)
         for k in range(dims.corners):
-            owners = jnp.where(corner == k, owner_ref[slot, k], owners)
+            if dims.coarse == 2:
+                owner = jnp.where(member == who, owner_ref[slot, k], others_ref[slot, k])
+            else:
+                owner = others_ref[who, slot, k]
+            owners = jnp.where(corner == k, owner, owners)
         hot.append(jnp.where(column == owners, 1.0, 0.0).astype(F32))
-    onehot = jnp.concatenate(hot, axis=0)
-    onehot_out[...] = onehot.astype(BF16)
-    inverse_out[...] = lax.dot_general(
+        own_hot.append(jnp.where(member == who, hot[-1], 0.0))
+    onto = jnp.dot(
+        jnp.concatenate(hot, axis=0),
         inverse_ref[0],
-        onehot,
+        precision=lax.Precision.HIGHEST,
+        preferred_element_type=F32,
+    )
+    between = lax.dot_general(
+        onto,
+        jnp.concatenate(own_hot, axis=0),
         (((1,), (1,)), ((), ())),
         precision=lax.Precision.HIGHEST,
         preferred_element_type=F32,
     )
+    pieces = jnp.concatenate(thirds(between), axis=0)
+    for slot in range(dims.slots):
+        lanes = slice(slot * dims.width, (slot + 1) * dims.width)
+        spread = jnp.dot(pieces, placed[slot], preferred_element_type=F32)
+        spread = (
+            spread[:corner_rows]
+            + spread[corner_rows : 2 * corner_rows]
+            + spread[2 * corner_rows :]
+        )
+        high, low = halves(spread)
+        high_out[:, lanes] = high
+        low_out[:, lanes] = low
     fetches[-1].wait()
 
 
@@ -187,6 +220,13 @@
     high = value.astype(BF16)
     low = (value - high.astype(F32)).astype(BF16)
     return high, low
+
+
+def thirds(value):
+    first = value.astype(BF16)
+    rest = value - first.astype(F32)
+    second, third = halves(rest)
+    return first, second, third
 
 
 def lane_sums(value):
@@ -205,24 +245,14 @@
             yield slot, block, value
 
 
-def coarse_part(dims, high_parts, low_parts, modes_ref, onehot_ref):
-    rows = dims.scen
+def corner_sums(dims, high_parts, low_parts, modes_ref):
     stacked = jnp.concatenate(
         [jnp.concatenate(high_parts, axis=1), jnp.concatenate(low_parts, axis=1)], axis=0
     )
     sums = lax.dot_general(
         stacked, modes_ref[...], (((1,), (1,)), ((), ())), preferred_element_type=F32
     )
-    sums = sums[:rows] + sums[rows:]
-    first, rest = halves(sums)
-    rest = sums - first.astype(F32)
-    second, third = halves(rest)
-    pieces = jnp.dot(
-        jnp.concatenate([first, second, third], axis=0),
-        onehot_ref[...],
-        preferred_element_type=F32,
-    )
-    return pieces[:rows] + pieces[rows : 2 * rows] + pieces[2 * rows :]
+    return sums[: dims.scen] + sums[dims.scen :]
 
 
 def jump_kernel(
@@ -233,9 +263,8 @@
     take_ref,
     weight_ref,
     modes_ref,
-    onehot_ref,
     jump_ref,
-    coarse_ref,
+    corner_ref,
 ):
     high_parts, low_parts = [], []
     for slot, block, value in jump_blocks(
@@ -245,7 +274,7 @@
         high, low = halves(value)
         high_parts.append(high)
         low_parts.append(low)
-    coarse_ref[...] = coarse_part(dims, high_parts, low_parts, modes_ref, onehot_ref)
+    corner_ref[...] = corner_sums(dims, high_parts, low_parts, modes_ref)
 
 
 def local_kernel(dims, direction_ref, flex_ref, out_ref):
@@ -278,19 +307,19 @@
     return tile
 
 
-def add_coarse(dims, local_ref, total, modes_ref, inverse_ref):
-    values = jnp.dot(
-        total, inverse_ref[...], precision=lax.Precision.HIGHEST, preferred_element_type=F32
-    )
-    high, low = halves(values)
-    both = jnp.dot(
-        jnp.concatenate([high, low], axis=0), modes_ref[...], preferred_element_type=F32
-    )
-    both = both[: dims.scen] + both[dims.scen :]
-    return [
-        local_ref[slot] + both[:, slot * dims.width : (slot + 1) * dims.width]
-        for slot in range(dims.slots)
-    ]
+def on_diagonal():
+    row = lax.broadcasted_iota(jnp.int32, (TILE, LANES), 0)
+    return row == lax.broadcasted_iota(jnp.int32, (TILE, LANES), 1)
+
+
+def add_coarse(dims, local_ref, sums, high_ref, low_ref):
+    high, low = halves(sums)
+    both = jnp.concatenate([high, low], axis=0)
+    for slot in range(dims.slots):
+        lanes = slice(slot * dims.width, (slot + 1) * dims.width)
+        part = jnp.dot(both, high_ref[:, lanes], preferred_element_type=F32)
+        rest = jnp.dot(high, low_ref[:, lanes], preferred_element_type=F32)
+        yield local_ref[slot] + (part[: dims.scen] + part[dims.scen :] + rest)
 
 
 def pack(dims, response, give_ref, near_ref, far_ref):
@@ -310,14 +339,14 @@
     local_ref,
     own_ref,
     other_ref,
-    modes_ref,
-    inverse_ref,
+    high_ref,
+    low_ref,
     give_ref,
     out_ref,
     near_ref,
     far_ref,
 ):
-    response = add_coarse(dims, local_ref, own_ref[...] + other_ref[...], modes_ref, inverse_ref)
+    response = list(add_coarse(dims, local_ref, own_ref[...] + other_ref[...], high_ref, low_ref))
     for slot in range(dims.slots):
         out_ref[slot] = response[slot]
     pack(dims, response, give_ref, near_ref, far_ref)
@@ -328,8 +357,8 @@
     local_ref,
     own_ref,
     other_ref,
-    modes_ref,
-    inverse_ref,
+    high_ref,
+    low_ref,
     give_ref,
     weight_ref,
     rhs_ref,
@@ -338,12 +367,13 @@
     out_ref,
     near_ref,
     far_ref,
+    sums_hbm,
     sums_ref,
+    sem,
 ):
-    response = add_coarse(dims, local_ref, own_ref[...] + other_ref[...], modes_ref, inverse_ref)
+    response = list(add_coarse(dims, local_ref, own_ref[...] + other_ref[...], high_ref, low_ref))
     acc = [jnp.zeros((dims.scen, LANES), F32)] * 2
     for slot in range(dims.slots):
-        out_ref[slot] = response[slot]
         for block in range(dims.blocks):
             place = slot * dims.blocks + block
             doubled = weight_ref[place, 1:2, :] * response[slot][
@@ -351,8 +381,16 @@
             ]
             acc[0] = acc[0] + block_of(rhs_ref, slot, block) * doubled
             acc[1] = acc[1] + block_of(image_ref, slot, block) * doubled
-    sums_ref[...] = jnp.broadcast_to((early_ref[...] + rows_of(acc, 3))[None], sums_ref.shape)
+    totals = jnp.sum(early_ref[...] + rows_of(acc, 3), axis=1, keepdims=True)
+    sums_ref[...] = jnp.broadcast_to(
+        lane_sums(jnp.where(on_diagonal(), totals, 0.0))[None], sums_ref.shape
+    )
+    put = pltpu.make_async_copy(sums_ref, sums_hbm, sem)
+    put.start()
+    for slot in range(dims.slots):
+        out_ref[slot] = response[slot]
     pack(dims, response, give_ref, near_ref, far_ref)
+    put.wait()
 
 
 def finish_kernel(
@@ -365,10 +403,14 @@
     far_ref,
     take_ref,
     weight_ref,
+    multiplier_hbm,
+    residual_hbm,
     multiplier_ref,
     residual_ref,
+    sems,
 ):
-    totals = jnp.sum(jnp.sum(sums_ref[...], axis=0), axis=1, keepdims=True)
+    row = jnp.sum(sums_ref[...], axis=0)
+    totals = jnp.sum(jnp.where(on_diagonal(), row, 0.0), axis=1, keepdims=True)
     norm, first, square, cross, second = (totals[q : q + 1, :] for q in range(5))
     step = norm / first
     norm_next = norm - 2.0 * step * first + step * step * square
@@ -377,6 +419,7 @@
     step_next = norm_next / curve
     on_first = step + step_next * grown
     on_second = step_next * step
+    puts = []
     for slot, block, second_image in jump_blocks(
         dims, field_ref, near_ref, far_ref, take_ref, weight_ref
     ):
@@ -385,6 +428,15 @@
         image = image_ref[slot, :, lanes]
         multiplier_ref[slot, :, lanes] = on_first * rhs - on_second * image
         residual_ref[slot, :, lanes] = rhs - on_first * image + on_second * second_image
+        if block + 1 == dims.blocks:
+            for i, (here, there) in enumerate(
+                ((multiplier_ref, multiplier_hbm), (residual_ref, residual_hbm))
+            ):
+                put = pltpu.make_async_copy(here.at[slot], there.at[slot], sems.at[i, slot])
+                put.start()
+                puts.append(put)
+    for put in puts:
+        put.wait()
 
 
 class Dims:
@@ -423,7 +475,7 @@
     whole = shape(free_response.shape, F32)
     packed = shape((SIDE, dims.scen, LANES), F32)
     per_block = shape((dims.per_device, TILE, LANES), F32)
-    corner_rows = dims.slots * dims.corners
+    corner_rows = dims.slots * dims.corners * dims.coarse
 
     near_pairs = [(d, d + 1 if d % 2 == 0 else d - 1) for d in range(dims.districts)]
     far_pairs = [
@@ -449,11 +501,15 @@
         scratch=[
             pltpu.SMEM(partner.shape, jnp.int32),
             pltpu.SMEM((2 * SIDE + 1,), jnp.int32),
-            pltpu.SemaphoreType.DMA((2,)),
+            pltpu.SemaphoreType.DMA((1 + dims.slots,)),
         ],
     )
     near, far = exchange(near, far)
-    take, give, weight, modes, onehot, inverse, flex = call(
+    if dims.coarse == 2:
+        others = lax.ppermute(corner_owner, "coarse", [(0, 1), (1, 0)])
+    else:
+        others = lax.all_gather(corner_owner, "coarse")
+    take, give, weight, modes, high, low, flex = call(
         prepare_kernel,
         dims,
         (
@@ -461,8 +517,8 @@
             per_block,
             per_block,
             shape((corner_rows, dims.slots * dims.width), BF16),
-            shape((corner_rows, dims.coarse_width), BF16),
-            shape((dims.coarse_width, corner_rows), F32),
+            shape((corner_rows, dims.slots * dims.width), BF16),
+            shape((corner_rows, dims.slots * dims.width), BF16),
             shape(flexibility.shape, BF16),
         ),
         tuple(
@@ -475,16 +531,18 @@
                 coarse_inverse,
                 flexibility,
             )
-        ),
-        in_specs=[HBM] * 6,
+        )
+        + (others,),
+        in_specs=[HBM] * 6 + [VMEM],
         scratch=[
             pltpu.SMEM(partner.shape, jnp.int32),
             pltpu.SMEM(iface_blocks.shape, jnp.int32),
             pltpu.SMEM(corner_owner.shape, jnp.int32),
             pltpu.VMEM(corner_modes.shape, BF16),
             pltpu.VMEM(coarse_inverse.shape, F32),
+            pltpu.SMEM(others.shape, jnp.int32),
             pltpu.SMEM((2 * SIDE + 1,), jnp.int32),
-            pltpu.SemaphoreType.DMA((6,)),
+            pltpu.SemaphoreType.DMA((7,)),
         ],
         cost=pl.CostEstimate(flops=10**7, bytes_accessed=4 * 10**6, transcendentals=0),
     )
@@ -493,8 +551,8 @@
         return call(
             jump_kernel,
             dims,
-            (whole, shape((dims.scen, dims.coarse_width), F32)),
-            (field, near, far, take, weight, modes, onehot),
+            (whole, shape((dims.scen, corner_rows), F32)),
+            (field, near, far, take, weight, modes),
         )
 
     matmul_cost = pl.CostEstimate(flops=10**8, bytes_accessed=3 * 10**6, transcendentals=0)
@@ -505,7 +563,7 @@
         respond_kernel,
         dims,
         (whole, packed, packed),
-        (term, part, other, modes, inverse, give),
+        (term, part, other, high, low, give),
     )
     near, far = exchange(near, far)
     image, part = jump(response, near, far)
@@ -520,8 +578,10 @@
     response, near, far, sums = call(
         respond_last_kernel,
         dims,
-        (whole, packed, packed, shape((devices, TILE, LANES), F32)),
-        (term, part, other, modes, inverse, give, weight, rhs, image, early),
+        (whole, packed, packed, shape((devices, 1, LANES), F32)),
+        (term, part, other, high, low, give, weight, rhs, image, early),
+        out_specs=(VMEM, VMEM, VMEM, HBM),
+        scratch=[pltpu.VMEM((devices, 1, LANES), F32), pltpu.SemaphoreType.DMA],
     )
     sums = lax.all_to_all(sums, AXES, 0, 0)
     near, far = exchange(near, far)
@@ -530,6 +590,12 @@
         dims,
         (whole, whole),
         (sums, rhs, image, response, near, far, take, weight),
+        out_specs=(HBM, HBM),
+        scratch=[
+            pltpu.VMEM(free_response.shape, F32),
+            pltpu.VMEM(free_response.shape, F32),
+            pltpu.SemaphoreType.DMA((2, dims.slots)),
+        ],
     )
 
 

time: 39.7 us -> 38.4 us (0.967)
  blocking collectives: 0 us -> 9.29 us
  starting transfers between devices: 23.2 us -> 15.6 us
  waiting for transfers between devices: 8.91 us -> 6.4 us
  Pallas kernels: 6.69 us -> 6.2 us
    all_to_all x0 -> x1, blocking collectives: none -> 9.29 us  [local(): sums = lax.all_to_all(sums, AXES, 0, 0)]
    all_to_all x1 -> x0, starting transfers between devices: 4.89 us -> none  [local(): sums = lax.all_to_all(sums, AXES, 0, 0)]
    ppermute x3, waiting for transfers between devices: 7.44 us -> 3.68 us  [exchange(): far = lax.ppermute(far, 'district', far_pairs)]
    ppermute x3, starting transfers between devices: 4.94 us -> 3.17 us  [exchange(): near = lax.ppermute(near, 'district', near_pairs)]
    ppermute x0 -> x1, waiting for transfers between devices: none -> 1.37 us  [local(): others = lax.ppermute(corner_owner, 'coarse', [(0, 1), (1, 0)])]
    ppermute x3, starting transfers between devices: 13.4 us -> 12.2 us  [exchange(): far = lax.ppermute(far, 'district', far_pairs)]
    pallas_call x9, Pallas kernels: 6.69 us -> 6.2 us  [call(): pl.pallas_call(functools.partial(kernel, dims), out_shape=outs, in_specs=...]
  transfers between devices with their start and end apart: 9 -> 9, of which waited for: 5 -> 5; matrix products, arithmetic and copies ran while one was open for 0% -> 0% of each run, Pallas kernels for 7% -> 8%
where the time goes in v1:
time: 38.4 us; the launch traced here: 38.2 us
  starting transfers between devices  15.6 us (41%)
  blocking collectives  9.29 us (24%)
  waiting for transfers between devices  6.4 us (17%)
  Pallas kernels  6.2 us (16%)
  between operations  0.7 us (2%)
    ppermute x3, starting transfers between devices, exchange(): far = lax.ppermute(far, 'district', far_pairs)  12.2 us
    all_to_all x1, blocking collectives, local(): sums = lax.all_to_all(sums, AXES, 0, 0)  9.29 us
    pallas_call x9, Pallas kernels, call(): pl.pallas_call(functools.partial(kernel, dims), out_shape=outs, in_specs=...  6.2 us
    ppermute x3, waiting for transfers between devices, exchange(): far = lax.ppermute(far, 'district', far_pairs)  3.68 us
    ppermute x3, starting transfers between devices, exchange(): near = lax.ppermute(near, 'district', near_pairs)  3.17 us
    ppermute x1, waiting for transfers between devices, local(): others = lax.ppermute(corner_owner, 'coarse', [(0, 1), (1, 0)])  1.37 us
    ppermute x2, waiting for transfers between devices, from_group(): return lax.ppermute(value, 'coarse', [(0, 1), (1, 0)])  1.28 us
  transfers between devices with their start and end apart: 9, of which 5 were waited for; matrix products, arithmetic and copies ran while one was open for 0% of the time, Pallas kernels for 8%

profile of v1, /device:TPU:0, one launch (start us, length us, event | category | flops | bytes accessed | tf_op | source)
XLA Modules:
  0.0 38.2 jit_solution(4644177542327211517)
XLA Ops:
  0.6 0.9 %shard_map.86 = (f32[4,16,128]{2,1,0:T(8,128)S(1)}, f32[4,16,128]{2,1,0:T(8,128)S(1)}, f32[4,16,512]{2,1,0:T(8,128)S(1)}) custom-call(s32[4,4]{1,0:T(4,128)} %partner_hbm.3, f32[4,16,512]{2,1,0:T(8,128)} %free_hbm.1), custom_call_target="tpu_custom_call" | custom-call | tf_op jit(solution)/shard_map/pallas_call | solution.py:451
  1.6 3.0 %collective-permute-start = (f32[4,16,128]{2,1,0:T(8,128)S(1)}, f32[4,16,128]{2,1,0:T(8,128)S(1)}, u32[]{:S(2)}, u32[]{:S(2)}) collective-permute-start(f32[4,16,128]{2,1,0:T(8,128)S(1)} %get-tuple-element.26), channel_id=1, source_target_pairs={{0,2},{2,0},{4,6},{6,4},{8,10},{10,8},{12,14},{14,12},{16,18},{18,... | collective-permute-start | bytes 98312 | tf_op jit(solution)/shard_map/ppermute | solution.py:487
  4.6 4.5 %collective-permute-start.1 = (f32[4,16,128]{2,1,0:T(8,128)S(1)}, f32[4,16,128]{2,1,0:T(8,128)S(1)}, u32[]{:S(2)}, u32[]{:S(2)}) collective-permute-start(f32[4,16,128]{2,1,0:T(8,128)S(1)} %get-tuple-element.27), channel_id=1, source_target_pairs={{0,30},{2,4},{4,2},{6,8},{8,6},{10,12},{12,10},{14,16},{16,14},{18... | collective-permute-start | bytes 98312 | tf_op jit(solution)/shard_map/ppermute | solution.py:486
  9.1 0.0 collective-permute-start.2
  9.1 1.4 %collective-permute-done.2.others_in = s32[4,8]{1,0:T(4,128)S(1)} collective-permute-done((s32[4,8]{1,0:T(4,128)}, s32[4,8]{1,0:T(4,128)S(1)}, u32[]{:S(2)}, u32[]{:S(2)}) %collective-permute-start.2) | collective-permute-done | bytes 160 | tf_op jit(solution)/shard_map/ppermute | solution.py:509
  10.5 2.3 %shard_map.87 = (f32[16,8,128]{2,1,0:T(8,128)S(1)}, f32[16,8,128]{2,1,0:T(8,128)S(1)}, f32[16,8,128]{2,1,0:T(8,128)S(1)}, bf16[64,2048]{1,0:T(8,128)(2,1)S(1)}, ...) custom-call(s32[4,4]{1,0:T(4,128)} %partner_hbm.3, s32[4]{0:T(128)} %iface_hbm.1, ...), custom_call_target="tpu_custom_call" | custom-call | flops 10000000 | bytes 4000000 | tf_op jit(solution)/shard_map/pallas_call | solution.py:451
  12.8 0.0 collective-permute-done.near_ref
  12.8 0.0 collective-permute-done.1.far_ref
  12.9 0.2 shard_map.88
  13.1 0.2 collective-permute-start.3
  13.3 0.4 %shard_map.89.local_ref = f32[4,16,512]{2,1,0:T(8,128)S(1)} custom-call(f32[4,16,512]{2,1,0:T(8,128)S(1)} %get-tuple-element.31.direction_ref.rhs_ref, bf16[4,512,512]{2,1,0:T(8,128)(2,1)S(1)} %get-tuple-element.32.flex_ref), custom_call_target="tpu_custom_call" | custom-call | flops 100000000 | bytes 3000000 | tf_op jit(solution)/shard_map/pallas_call | solution.py:451
  13.7 0.6 %collective-permute-done.3.other_ref = f32[16,64]{1,0:T(8,128)S(1)} collective-permute-done((f32[16,64]{1,0:T(8,128)S(1)}, f32[16,64]{1,0:T(8,128)S(1)}, u32[]{:S(2)}, u32[]{:S(2)}) %collective-permute-start.3) | collective-permute-done | bytes 4128 | tf_op jit(solution)/shard_map/ppermute | solution.py:492
  14.3 0.2 shard_map.90
  14.5 0.1 collective-permute-start.4
  14.6 3.8 %collective-permute-start.5 = (f32[4,16,128]{2,1,0:T(8,128)S(1)}, f32[4,16,128]{2,1,0:T(8,128)S(1)}, u32[]{:S(2)}, u32[]{:S(2)}) collective-permute-start(f32[4,16,128]{2,1,0:T(8,128)S(1)} %get-tuple-element.39), channel_id=1, source_target_pairs={{0,30},{2,4},{4,2},{6,8},{8,6},{10,12},{12,10},{14,16},{16,14},{18... | collective-permute-start | bytes 98312 | tf_op jit(solution)/shard_map/ppermute | solution.py:486
  18.4 0.1 collective-permute-done.4.near_ref
  18.5 3.7 %collective-permute-done.5.far_ref = f32[4,16,128]{2,1,0:T(8,128)S(1)} collective-permute-done((f32[4,16,128]{2,1,0:T(8,128)S(1)}, f32[4,16,128]{2,1,0:T(8,128)S(1)}, u32[]{:S(2)}, u32[]{:S(2)}) %collective-permute-start.5) | collective-permute-done | bytes 32800 | tf_op jit(solution)/shard_map/ppermute | solution.py:486
  22.2 0.2 shard_map.91
  22.4 0.0 collective-permute-start.6
  22.4 0.5 %shard_map.92 = (f32[4,16,512]{2,1,0:T(8,128)S(1)}, f32[8,128]{1,0:T(8,128)S(1)}) custom-call(f32[4,16,512]{2,1,0:T(8,128)S(1)} %get-tuple-element.40.direction_ref.image_ref, bf16[4,512,512]{2,1,0:T(8,128)(2,1)S(1)} %get-tuple-element.32.flex_ref, f32[4,16,512]{2,1,0:T(8,128)S(1)} %get-tuple-element.31.direction_ref.rhs_ref), custom_call_target="tpu_custom_call" | custom-call | flops 100000000 | bytes 3000000 | tf_op jit(solution)/shard_map/pallas_call | solution.py:451
  22.8 0.7 %collective-permute-done.6.other_ref = f32[16,64]{1,0:T(8,128)S(1)} collective-permute-done((f32[16,64]{1,0:T(8,128)S(1)}, f32[16,64]{1,0:T(8,128)S(1)}, u32[]{:S(2)}, u32[]{:S(2)}) %collective-permute-start.6) | collective-permute-done | bytes 4128 | tf_op jit(solution)/shard_map/ppermute | solution.py:492
  23.6 0.4 %shard_map.93 = (f32[4,16,512]{2,1,0:T(8,128)S(1)}, f32[4,16,128]{2,1,0:T(8,128)S(1)}, f32[4,16,128]{2,1,0:T(8,128)S(1)}, f32[32,1,128]{2,1,0:T(1,128)S(1)}) custom-call(f32[4,16,512]{2,1,0:T(8,128)S(1)} %get-tuple-element.41.local_ref, f32[16,64]{1,0:T(8,128)S(1)} %get-tuple-element.42.own_ref, f32[16,64]{1,0:T(8,128)S(1)} %collective-permute-done.6.other_ref, ...), custom_call_target="tpu_custom_call" | custom-call | tf_op jit(solution)/shard_map/pallas_call | solution.py:451
  24.0 0.1 collective-permute-start.7
  24.1 3.8 %collective-permute-start.8 = (f32[4,16,128]{2,1,0:T(8,128)S(1)}, f32[4,16,128]{2,1,0:T(8,128)S(1)}, u32[]{:S(2)}, u32[]{:S(2)}) collective-permute-start(f32[4,16,128]{2,1,0:T(8,128)S(1)} %get-tuple-element.47), channel_id=1, source_target_pairs={{0,30},{2,4},{4,2},{6,8},{8,6},{10,12},{12,10},{14,16},{16,14},{18... | collective-permute-start | bytes 98312 | tf_op jit(solution)/shard_map/ppermute | solution.py:486
  27.9 9.3 %all_to_all.5.sums_ref = f32[32,1,128]{2,1,0:T(1,128)S(1)} all-to-all(f32[32,1,128]{2,1,0:T(1,128)S(1)} %get-tuple-element.44), channel_id=1, replica_groups=mesh['district'=16,'coarse'=2] {'district','coarse'}, dimensions={0} | all-to-all | bytes 32768 | tf_op jit(solution)/shard_map/all_to_all | solution.py:586
  37.2 0.0 collective-permute-done.7.near_ref
  37.2 0.0 collective-permute-done.8.far_ref
  37.2 0.9 %shard_map.94 = (f32[4,16,512]{2,1,0:T(8,128)}, f32[4,16,512]{2,1,0:T(8,128)}) custom-call(f32[32,1,128]{2,1,0:T(1,128)S(1)} %all_to_all.5.sums_ref, f32[4,16,512]{2,1,0:T(8,128)S(1)} %get-tuple-element.31.direction_ref.rhs_ref, f32[4,16,512]{2,1,0:T(8,128)S(1)} %get-tuple-element.40.direction_ref.image_ref, f32[4,16,512]{2,1,0:T(8,128)S(1)} %get-tuple-element.45.field_ref, ...), custom_call_target="tpu_custom_call" | custom-call | tf_op jit(solution)/shard_map/pallas_call | solution.py:451
Async XLA Ops:
  1.6 11.3 %collective-permute-start = (f32[4,16,128]{2,1,0:T(8,128)S(1)}, f32[4,16,128]{2,1,0:T(8,128)S(1)}, u32[]{:S(2)}, u32[]{:S(2)}) collective-permute-start(f32[4,16,128]{2,1,0:T(8,128)S(1)} %get-tuple-element.26), channel_id=1, source_target_pairs={{0,2},{2,0},{4,6},{6,4},{8,10},{10,8},{12,14},{14,12},{16,18},{18,... | collective-permute-start | bytes 98312 | tf_op jit(solution)/shard_map/ppermute | solution.py:487
  4.6 8.2 %collective-permute-start.1 = (f32[4,16,128]{2,1,0:T(8,128)S(1)}, f32[4,16,128]{2,1,0:T(8,128)S(1)}, u32[]{:S(2)}, u32[]{:S(2)}) collective-permute-start(f32[4,16,128]{2,1,0:T(8,128)S(1)} %get-tuple-element.27), channel_id=1, source_target_pairs={{0,30},{2,4},{4,2},{6,8},{8,6},{10,12},{12,10},{14,16},{16,14},{18... | collective-permute-start | bytes 98312 | tf_op jit(solution)/shard_map/ppermute | solution.py:486
  9.1 1.4 %collective-permute-start.2 = (s32[4,8]{1,0:T(4,128)}, s32[4,8]{1,0:T(4,128)S(1)}, u32[]{:S(2)}, u32[]{:S(2)}) collective-permute-start(s32[4,8]{1,0:T(4,128)} %owner_hbm.1), channel_id=1, source_target_pairs={{0,1},{1,0},{2,3},{3,2},{4,5},{5,4},{6,7},{7,6},{8,9},{9,8},{10,11... | collective-permute-start | bytes 392 | tf_op jit(solution)/shard_map/ppermute | solution.py:509
  13.1 1.2 %collective-permute-start.3 = (f32[16,64]{1,0:T(8,128)S(1)}, f32[16,64]{1,0:T(8,128)S(1)}, u32[]{:S(2)}, u32[]{:S(2)}) collective-permute-start(f32[16,64]{1,0:T(8,128)S(1)} %get-tuple-element.33.own_ref), channel_id=1, source_target_pairs={{0,1},{1,0},{2,3},{3,2},{4,5},{5,4},{6,7},{7,6},{8,9},{9,8},{10,11... | collective-permute-start | bytes 12296 | tf_op jit(solution)/shard_map/ppermute | solution.py:492
  14.5 4.0 %collective-permute-start.4 = (f32[4,16,128]{2,1,0:T(8,128)S(1)}, f32[4,16,128]{2,1,0:T(8,128)S(1)}, u32[]{:S(2)}, u32[]{:S(2)}) collective-permute-start(f32[4,16,128]{2,1,0:T(8,128)S(1)} %get-tuple-element.38), channel_id=1, source_target_pairs={{0,2},{2,0},{4,6},{6,4},{8,10},{10,8},{12,14},{14,12},{16,18},{18,... | collective-permute-start | bytes 98312 | tf_op jit(solution)/shard_map/ppermute | solution.py:487
  14.6 7.6 %collective-permute-start.5 = (f32[4,16,128]{2,1,0:T(8,128)S(1)}, f32[4,16,128]{2,1,0:T(8,128)S(1)}, u32[]{:S(2)}, u32[]{:S(2)}) collective-permute-start(f32[4,16,128]{2,1,0:T(8,128)S(1)} %get-tuple-element.39), channel_id=1, source_target_pairs={{0,30},{2,4},{4,2},{6,8},{8,6},{10,12},{12,10},{14,16},{16,14},{18... | collective-permute-start | bytes 98312 | tf_op jit(solution)/shard_map/ppermute | solution.py:486
  22.4 1.2 %collective-permute-start.6 = (f32[16,64]{1,0:T(8,128)S(1)}, f32[16,64]{1,0:T(8,128)S(1)}, u32[]{:S(2)}, u32[]{:S(2)}) collective-permute-start(f32[16,64]{1,0:T(8,128)S(1)} %get-tuple-element.42.own_ref), channel_id=1, source_target_pairs={{0,1},{1,0},{2,3},{3,2},{4,5},{5,4},{6,7},{7,6},{8,9},{9,8},{10,11... | collective-permute-start | bytes 12296 | tf_op jit(solution)/shard_map/ppermute | solution.py:492
  24.0 13.2 %collective-permute-start.7 = (f32[4,16,128]{2,1,0:T(8,128)S(1)}, f32[4,16,128]{2,1,0:T(8,128)S(1)}, u32[]{:S(2)}, u32[]{:S(2)}) collective-permute-start(f32[4,16,128]{2,1,0:T(8,128)S(1)} %get-tuple-element.46), channel_id=1, source_target_pairs={{0,2},{2,0},{4,6},{6,4},{8,10},{10,8},{12,14},{14,12},{16,18},{18,... | collective-permute-start | bytes 98312 | tf_op jit(solution)/shard_map/ppermute | solution.py:487
  24.1 13.1 %collective-permute-start.8 = (f32[4,16,128]{2,1,0:T(8,128)S(1)}, f32[4,16,128]{2,1,0:T(8,128)S(1)}, u32[]{:S(2)}, u32[]{:S(2)}) collective-permute-start(f32[4,16,128]{2,1,0:T(8,128)S(1)} %get-tuple-element.47), channel_id=1, source_target_pairs={{0,30},{2,4},{4,2},{6,8},{8,6},{10,12},{12,10},{14,16},{16,14},{18... | collective-permute-start | bytes 98312 | tf_op jit(solution)/shard_map/ppermute | solution.py:486

commit v2 on v1

--- a/solution.py
+++ b/solution.py
@@ -30,6 +30,12 @@
     return lax.rem(value, jnp.int32(by))
 
 
+def group_of(place, size):
+    if size & (size - 1) == 0:
+        return lax.shift_right_arithmetic(place, jnp.int32(size.bit_length() - 1))
+    return jnp.where(place < 0, -1, lax.div(place, jnp.int32(size)))
+
+
 def near_side(index):
     return jnp.where(remainder(index, 2) == 0, index + 1, index - 1)
 
@@ -50,14 +56,12 @@
     for slot in range(dims.slots):
         for block in range(dims.blocks):
             place = partner_ref[slot, block]
-            paired = place >= 0
-            safe = jnp.maximum(place, 0)
-            district = quotient(safe, dims.coarse * dims.per_device)
+            district = group_of(place, dims.coarse * dims.per_device)
             out.append(
                 (
-                    jnp.logical_and(paired, district == near).astype(jnp.int32),
-                    jnp.logical_and(paired, district == far).astype(jnp.int32),
-                    remainder(safe, dims.per_device),
+                    (district == near).astype(jnp.int32),
+                    (district == far).astype(jnp.int32),
+                    place,
                 )
             )
     return out
@@ -143,13 +147,14 @@
     row = lax.broadcasted_iota(jnp.int32, (TILE, LANES), 0)
     near_count = jnp.int32(0)
     far_count = jnp.int32(0)
-    for place, (near, far, other) in enumerate(faces):
+    for place, (near, far, whole) in enumerate(faces):
         slot = jnp.where(near > 0, near_count, jnp.where(far > 0, SIDE + far_count, 2 * SIDE))
-        partners[slot] = other
+        partners[slot] = remainder(jnp.maximum(whole, 0), dims.per_device)
         give_ref[place] = jnp.where(row == slot, 1.0, 0.0).astype(F32)
         near_count += near
         far_count += far
-    for place, (near, far, other) in enumerate(faces):
+    for place, (near, far, whole) in enumerate(faces):
+        other = remainder(jnp.maximum(whole, 0), dims.per_device)
         slot_id, block_id = divmod(place, dims.blocks)
         from_near = jnp.int32(0)
         from_far = jnp.int32(SIDE)
@@ -233,12 +238,12 @@
     return jnp.sum(value, axis=0, keepdims=True)
 
 
-def jump_blocks(dims, field_ref, near_ref, far_ref, take_ref, weight_ref):
+def jump_blocks(dims, field_ref, sides, take_ref, weight_ref):
     for slot in range(dims.slots):
         for block in range(dims.blocks):
             place = slot * dims.blocks + block
             value = block_of(field_ref, slot, block) * weight_ref[place, 0:1, :]
-            for side, ref in enumerate((near_ref, far_ref)):
+            for side, ref in enumerate(sides):
                 for j in range(SIDE):
                     row = side * SIDE + j
                     value = value - take_ref[place, row : row + 1, :] * ref[j]
@@ -268,7 +273,7 @@
 ):
     high_parts, low_parts = [], []
     for slot, block, value in jump_blocks(
-        dims, field_ref, near_ref, far_ref, take_ref, weight_ref
+        dims, field_ref, (near_ref, far_ref), take_ref, weight_ref
     ):
         jump_ref[slot, :, block * LANES : (block + 1) * LANES] = value
         high, low = halves(value)
@@ -277,31 +282,77 @@
     corner_ref[...] = corner_sums(dims, high_parts, low_parts, modes_ref)
 
 
-def local_kernel(dims, direction_ref, flex_ref, out_ref):
+def local_term(dims, direction_ref, flex_ref):
     for slot in range(dims.slots):
         high, low = halves(direction_ref[slot])
         both = jnp.dot(
             jnp.concatenate([high, low], axis=0), flex_ref[slot], preferred_element_type=F32
         )
-        out_ref[slot] = both[: dims.scen] + both[dims.scen :]
-
-
-def local_last_kernel(dims, direction_ref, flex_ref, rhs_ref, out_ref, sums_ref):
-    local_kernel(dims, direction_ref, flex_ref, out_ref)
-    acc = [jnp.zeros((dims.scen, LANES), F32)] * 3
-    for slot in range(dims.slots):
+        yield both[: dims.scen] + both[dims.scen :]
+
+
+def corner_weights(dims, field_ref, weight_ref, high_ref, low_ref):
+    high_parts, low_parts = [], []
+    for slot in range(dims.slots):
+        for block in range(dims.blocks):
+            place = slot * dims.blocks + block
+            value = block_of(field_ref, slot, block) * weight_ref[place, 1:2, :]
+            high, low = halves(value)
+            high_parts.append(high)
+            low_parts.append(low)
+    high = jnp.concatenate(high_parts, axis=1)
+    both = jnp.concatenate([high, jnp.concatenate(low_parts, axis=1)], axis=0)
+    contract = (((1,), (1,)), ((), ()))
+    part = lax.dot_general(both, high_ref[...], contract, preferred_element_type=F32)
+    rest = lax.dot_general(high, low_ref[...], contract, preferred_element_type=F32)
+    return part[: dims.scen] + part[dims.scen :] + rest
+
+
+def local_kernel(dims, direction_ref, flex_ref, weight_ref, high_ref, low_ref, out_ref, g_ref):
+    for slot, term in enumerate(local_term(dims, direction_ref, flex_ref)):
+        out_ref[slot] = term
+    g_ref[...] = corner_weights(dims, direction_ref, weight_ref, high_ref, low_ref)
+
+
+def local_last_kernel(
+    dims,
+    direction_ref,
+    flex_ref,
+    weight_ref,
+    high_ref,
+    low_ref,
+    rhs_ref,
+    out_ref,
+    g_ref,
+    sums_ref,
+):
+    acc = [jnp.zeros((dims.scen, LANES), F32)] * 5
+    for slot, term in enumerate(local_term(dims, direction_ref, flex_ref)):
+        out_ref[slot] = term
         for block in range(dims.blocks):
             rhs = block_of(rhs_ref, slot, block)
             image = block_of(direction_ref, slot, block)
-            acc[0] = acc[0] + rhs * rhs
-            acc[1] = acc[1] + rhs * image
-            acc[2] = acc[2] + image * image
-    sums_ref[...] = rows_of(acc, 0)
+            doubled = (
+                weight_ref[slot * dims.blocks + block, 1:2, :]
+                * term[:, block * LANES : (block + 1) * LANES]
+            )
+            for q, product in enumerate(
+                (rhs * rhs, rhs * image, image * image, rhs * doubled, image * doubled)
+            ):
+                acc[q] = acc[q] + product
+    sums_ref[...] = totals_of(rows_of(acc, 0))
+    g_ref[...] = corner_weights(dims, direction_ref, weight_ref, high_ref, low_ref)
+
+
+def totals_of(tile):
+    totals = jnp.sum(tile, axis=1, keepdims=True)
+    return lane_sums(jnp.where(on_diagonal(), totals, 0.0))
 
 
 def rows_of(parts, first):
-    row = lax.broadcasted_iota(jnp.int32, (TILE, LANES), 0)
-    tile = jnp.zeros((TILE, LANES), F32)
+    lanes = parts[0].shape[1]
+    row = lax.broadcasted_iota(jnp.int32, (TILE, lanes), 0)
+    tile = jnp.zeros((TILE, lanes), F32)
     for q, part in enumerate(parts):
         tile = jnp.where(row == first + q, lane_sums(part), tile)
     return tile
@@ -360,9 +411,8 @@
     high_ref,
     low_ref,
     give_ref,
-    weight_ref,
-    rhs_ref,
-    image_ref,
+    rhs_g_ref,
+    image_g_ref,
     early_ref,
     out_ref,
     near_ref,
@@ -371,45 +421,32 @@
     sums_ref,
     sem,
 ):
-    response = list(add_coarse(dims, local_ref, own_ref[...] + other_ref[...], high_ref, low_ref))
-    acc = [jnp.zeros((dims.scen, LANES), F32)] * 2
-    for slot in range(dims.slots):
-        for block in range(dims.blocks):
-            place = slot * dims.blocks + block
-            doubled = weight_ref[place, 1:2, :] * response[slot][
-                :, block * LANES : (block + 1) * LANES
-            ]
-            acc[0] = acc[0] + block_of(rhs_ref, slot, block) * doubled
-            acc[1] = acc[1] + block_of(image_ref, slot, block) * doubled
-    totals = jnp.sum(early_ref[...] + rows_of(acc, 3), axis=1, keepdims=True)
-    sums_ref[...] = jnp.broadcast_to(
-        lane_sums(jnp.where(on_diagonal(), totals, 0.0))[None], sums_ref.shape
-    )
+    corner = own_ref[...] + other_ref[...]
+    late = totals_of(rows_of((corner * rhs_g_ref[...], corner * image_g_ref[...]), 3))
+    sums_ref[...] = jnp.broadcast_to((early_ref[...] + late)[None], sums_ref.shape)
     put = pltpu.make_async_copy(sums_ref, sums_hbm, sem)
     put.start()
+    response = list(add_coarse(dims, local_ref, corner, high_ref, low_ref))
     for slot in range(dims.slots):
         out_ref[slot] = response[slot]
     pack(dims, response, give_ref, near_ref, far_ref)
     put.wait()
 
 
-def finish_kernel(
+def settle_kernel(
     dims,
     sums_ref,
     rhs_ref,
     image_ref,
     field_ref,
     near_ref,
-    far_ref,
     take_ref,
     weight_ref,
-    multiplier_hbm,
-    residual_hbm,
     multiplier_ref,
     residual_ref,
-    sems,
-):
-    row = jnp.sum(sums_ref[...], axis=0)
+    factor_ref,
+):
+    row = lane_sums(sums_ref[...])
     totals = jnp.sum(jnp.where(on_diagonal(), row, 0.0), axis=1, keepdims=True)
     norm, first, square, cross, second = (totals[q : q + 1, :] for q in range(5))
     step = norm / first
@@ -419,22 +456,50 @@
     step_next = norm_next / curve
     on_first = step + step_next * grown
     on_second = step_next * step
-    puts = []
+    factor_ref[...] = jnp.broadcast_to(on_second, factor_ref.shape)
     for slot, block, second_image in jump_blocks(
-        dims, field_ref, near_ref, far_ref, take_ref, weight_ref
+        dims, field_ref, (near_ref,), take_ref, weight_ref
     ):
         lanes = slice(block * LANES, (block + 1) * LANES)
         rhs = rhs_ref[slot, :, lanes]
         image = image_ref[slot, :, lanes]
         multiplier_ref[slot, :, lanes] = on_first * rhs - on_second * image
         residual_ref[slot, :, lanes] = rhs - on_first * image + on_second * second_image
-        if block + 1 == dims.blocks:
-            for i, (here, there) in enumerate(
-                ((multiplier_ref, multiplier_hbm), (residual_ref, residual_hbm))
-            ):
-                put = pltpu.make_async_copy(here.at[slot], there.at[slot], sems.at[i, slot])
-                put.start()
-                puts.append(put)
+
+
+def finish_kernel(
+    dims,
+    multiplier_ref,
+    partial_ref,
+    factor_ref,
+    far_ref,
+    take_ref,
+    multiplier_hbm,
+    residual_hbm,
+    residual_ref,
+    sems,
+):
+    puts = [
+        pltpu.make_async_copy(
+            multiplier_ref.at[slot], multiplier_hbm.at[slot], sems.at[0, slot]
+        )
+        for slot in range(dims.slots)
+    ]
+    for put in puts:
+        put.start()
+    factor = factor_ref[0:1, :]
+    sides = [factor * far_ref[j] for j in range(SIDE)]
+    for slot in range(dims.slots):
+        for block in range(dims.blocks):
+            place = slot * dims.blocks + block
+            lanes = slice(block * LANES, (block + 1) * LANES)
+            value = partial_ref[slot, :, lanes]
+            for j in range(SIDE):
+                value = value - take_ref[place, SIDE + j : SIDE + j + 1, :] * sides[j]
+            residual_ref[slot, :, lanes] = value
+        put = pltpu.make_async_copy(residual_ref.at[slot], residual_hbm.at[slot], sems.at[1, slot])
+        put.start()
+        puts.append(put)
     for put in puts:
         put.wait()
 
@@ -558,7 +623,14 @@
     matmul_cost = pl.CostEstimate(flops=10**8, bytes_accessed=3 * 10**6, transcendentals=0)
     rhs, part = jump(field, near, far)
     other = from_group(part)
-    term = call(local_kernel, dims, whole, (rhs, flex), cost=matmul_cost)
+    corners = shape((dims.scen, corner_rows), F32)
+    term, rhs_g = call(
+        local_kernel,
+        dims,
+        (whole, corners),
+        (rhs, flex, weight, high, low),
+        cost=matmul_cost,
+    )
     response, near, far = call(
         respond_kernel,
         dims,
@@ -568,34 +640,36 @@
     near, far = exchange(near, far)
     image, part = jump(response, near, far)
     other = from_group(part)
-    term, early = call(
+    term, image_g, early = call(
         local_last_kernel,
         dims,
-        (whole, shape((TILE, LANES), F32)),
-        (image, flex, rhs),
+        (whole, corners, shape((1, LANES), F32)),
+        (image, flex, weight, high, low, rhs),
         cost=matmul_cost,
     )
     response, near, far, sums = call(
         respond_last_kernel,
         dims,
         (whole, packed, packed, shape((devices, 1, LANES), F32)),
-        (term, part, other, high, low, give, weight, rhs, image, early),
+        (term, part, other, high, low, give, rhs_g, image_g, early),
         out_specs=(VMEM, VMEM, VMEM, HBM),
         scratch=[pltpu.VMEM((devices, 1, LANES), F32), pltpu.SemaphoreType.DMA],
     )
     sums = lax.all_to_all(sums, AXES, 0, 0)
     near, far = exchange(near, far)
+    multiplier, residual, factor = call(
+        settle_kernel,
+        dims,
+        (whole, whole, shape((TILE, LANES), F32)),
+        (sums.reshape(devices, LANES), rhs, image, response, near, take, weight),
+    )
     return call(
         finish_kernel,
         dims,
         (whole, whole),
-        (sums, rhs, image, response, near, far, take, weight),
+        (multiplier, residual, factor, far, take),
         out_specs=(HBM, HBM),
-        scratch=[
-            pltpu.VMEM(free_response.shape, F32),
-            pltpu.VMEM(free_response.shape, F32),
-            pltpu.SemaphoreType.DMA((2, dims.slots)),
-        ],
+        scratch=[pltpu.VMEM(free_response.shape, F32), pltpu.SemaphoreType.DMA((2, dims.slots))],
     )
 
 

time: 38.4 us -> 38.3 us (level)
    pallas_call x9 -> x10, Pallas kernels: 6.2 us -> 6.4 us  [call(): pl.pallas_call(functools.partial(kernel, dims), out_shape=outs, in_specs=...]
  transfers between devices with their start and end apart: 9 -> 9, of which waited for: 5 -> 4; matrix products, arithmetic and copies ran while one was open for 0% -> 0% of each run, Pallas kernels for 8% -> 10%
where the time goes in v2:
time: 38.3 us; the launch traced here: 38.1 us
  starting transfers between devices  15.6 us (41%)
  blocking collectives  9.29 us (24%)
  Pallas kernels  6.4 us (17%)
  waiting for transfers between devices  6.04 us (16%)
  between operations  0.72 us (2%)
    ppermute x3, starting transfers between devices, exchange(): far = lax.ppermute(far, 'district', far_pairs)  12.3 us
    all_to_all x1, blocking collectives, local(): sums = lax.all_to_all(sums, AXES, 0, 0)  9.29 us
    pallas_call x10, Pallas kernels, call(): pl.pallas_call(functools.partial(kernel, dims), out_shape=outs, in_specs=...  6.4 us
    ppermute x3, waiting for transfers between devices, exchange(): far = lax.ppermute(far, 'district', far_pairs)  3.68 us
    ppermute x3, starting transfers between devices, exchange(): near = lax.ppermute(near, 'district', near_pairs)  3.17 us
    ppermute x1, waiting for transfers between devices, local(): others = lax.ppermute(corner_owner, 'coarse', [(0, 1), (1, 0)])  1.37 us
    ppermute x2, waiting for transfers between devices, from_group(): return lax.ppermute(value, 'coarse', [(0, 1), (1, 0)])  0.95 us
  transfers between devices with their start and end apart: 9, of which 4 were waited for; matrix products, arithmetic and copies ran while one was open for 0% of the time, Pallas kernels for 10%

profile of v2, /device:TPU:0, one launch (start us, length us, event | category | flops | bytes accessed | tf_op | source)
XLA Modules:
  0.0 38.1 jit_solution(12422084565951913463)
XLA Ops:
  0.6 0.9 %shard_map.86 = (f32[4,16,128]{2,1,0:T(8,128)S(1)}, f32[4,16,128]{2,1,0:T(8,128)S(1)}, f32[4,16,512]{2,1,0:T(8,128)S(1)}) custom-call(s32[4,4]{1,0:T(4,128)} %partner_hbm.3, f32[4,16,512]{2,1,0:T(8,128)} %free_hbm.1), custom_call_target="tpu_custom_call" | custom-call | tf_op jit(solution)/shard_map/pallas_call | solution.py:516
  1.5 3.0 %collective-permute-start = (f32[4,16,128]{2,1,0:T(8,128)S(1)}, f32[4,16,128]{2,1,0:T(8,128)S(1)}, u32[]{:S(2)}, u32[]{:S(2)}) collective-permute-start(f32[4,16,128]{2,1,0:T(8,128)S(1)} %get-tuple-element.32), channel_id=1, source_target_pairs={{0,2},{2,0},{4,6},{6,4},{8,10},{10,8},{12,14},{14,12},{16,18},{18,... | collective-permute-start | bytes 98312 | tf_op jit(solution)/shard_map/ppermute | solution.py:552
  4.5 4.5 %collective-permute-start.1 = (f32[4,16,128]{2,1,0:T(8,128)S(1)}, f32[4,16,128]{2,1,0:T(8,128)S(1)}, u32[]{:S(2)}, u32[]{:S(2)}) collective-permute-start(f32[4,16,128]{2,1,0:T(8,128)S(1)} %get-tuple-element.33), channel_id=1, source_target_pairs={{0,30},{2,4},{4,2},{6,8},{8,6},{10,12},{12,10},{14,16},{16,14},{18... | collective-permute-start | bytes 98312 | tf_op jit(solution)/shard_map/ppermute | solution.py:551
  9.1 0.0 collective-permute-start.2
  9.1 1.4 %collective-permute-done.2.others_in = s32[4,8]{1,0:T(4,128)S(1)} collective-permute-done((s32[4,8]{1,0:T(4,128)}, s32[4,8]{1,0:T(4,128)S(1)}, u32[]{:S(2)}, u32[]{:S(2)}) %collective-permute-start.2) | collective-permute-done | bytes 160 | tf_op jit(solution)/shard_map/ppermute | solution.py:574
  10.4 2.3 %shard_map.87 = (f32[16,8,128]{2,1,0:T(8,128)S(1)}, f32[16,8,128]{2,1,0:T(8,128)S(1)}, f32[16,8,128]{2,1,0:T(8,128)S(1)}, bf16[64,2048]{1,0:T(8,128)(2,1)S(1)}, ...) custom-call(s32[4,4]{1,0:T(4,128)} %partner_hbm.3, s32[4]{0:T(128)} %iface_hbm.1, ...), custom_call_target="tpu_custom_call" | custom-call | flops 10000000 | bytes 4000000 | tf_op jit(solution)/shard_map/pallas_call | solution.py:516
  12.8 0.0 collective-permute-done.near_ref
  12.8 0.0 collective-permute-done.1.far_ref
  12.8 0.2 shard_map.88
  13.0 0.2 collective-permute-start.3
  13.2 0.6 %shard_map.89 = (f32[4,16,512]{2,1,0:T(8,128)S(1)}, f32[16,64]{1,0:T(8,128)S(1)}) custom-call(f32[4,16,512]{2,1,0:T(8,128)S(1)} %get-tuple-element.37.direction_ref.rhs_ref, bf16[4,512,512]{2,1,0:T(8,128)(2,1)S(1)} %get-tuple-element.38.flex_ref, f32[16,8,128]{2,1,0:T(8,128)S(1)} %get-tuple-element.35.weight_ref, ...), custom_call_target="tpu_custom_call" | custom-call | flops 100000000 | bytes 3000000 | tf_op jit(solution)/shard_map/pallas_call | solution.py:516
  13.7 0.5 %collective-permute-done.3.other_ref = f32[16,64]{1,0:T(8,128)S(1)} collective-permute-done((f32[16,64]{1,0:T(8,128)S(1)}, f32[16,64]{1,0:T(8,128)S(1)}, u32[]{:S(2)}, u32[]{:S(2)}) %collective-permute-start.3) | collective-permute-done | bytes 4128 | tf_op jit(solution)/shard_map/ppermute | solution.py:557
  14.2 0.2 shard_map.90
  14.4 0.1 collective-permute-start.4
  14.5 3.9 %collective-permute-start.5 = (f32[4,16,128]{2,1,0:T(8,128)S(1)}, f32[4,16,128]{2,1,0:T(8,128)S(1)}, u32[]{:S(2)}, u32[]{:S(2)}) collective-permute-start(f32[4,16,128]{2,1,0:T(8,128)S(1)} %get-tuple-element.46), channel_id=1, source_target_pairs={{0,30},{2,4},{4,2},{6,8},{8,6},{10,12},{12,10},{14,16},{16,14},{18... | collective-permute-start | bytes 98312 | tf_op jit(solution)/shard_map/ppermute | solution.py:551
  18.4 0.0 collective-permute-done.4.near_ref
  18.4 3.7 %collective-permute-done.5.far_ref = f32[4,16,128]{2,1,0:T(8,128)S(1)} collective-permute-done((f32[4,16,128]{2,1,0:T(8,128)S(1)}, f32[4,16,128]{2,1,0:T(8,128)S(1)}, u32[]{:S(2)}, u32[]{:S(2)}) %collective-permute-start.5) | collective-permute-done | bytes 32800 | tf_op jit(solution)/shard_map/ppermute | solution.py:551
  22.1 0.2 shard_map.91
  22.3 0.0 collective-permute-start.6
  22.3 0.7 %shard_map.92 = (f32[4,16,512]{2,1,0:T(8,128)S(1)}, f32[16,64]{1,0:T(8,128)S(1)}, f32[1,128]{1,0:T(1,128)S(1)}) custom-call(f32[4,16,512]{2,1,0:T(8,128)S(1)} %get-tuple-element.47.direction_ref.image_ref, bf16[4,512,512]{2,1,0:T(8,128)(2,1)S(1)} %get-tuple-element.38.flex_ref, f32[16,8,128]{2,1,0:T(8,128)S(1)} %get-tuple-element.35.weight_ref, ...), custom_call_target="tpu_custom_call" | custom-call | flops 100000000 | bytes 3000000 | tf_op jit(solution)/shard_map/pallas_call | solution.py:516
  23.0 0.5 %collective-permute-done.6.other_ref = f32[16,64]{1,0:T(8,128)S(1)} collective-permute-done((f32[16,64]{1,0:T(8,128)S(1)}, f32[16,64]{1,0:T(8,128)S(1)}, u32[]{:S(2)}, u32[]{:S(2)}) %collective-permute-start.6) | collective-permute-done | bytes 4128 | tf_op jit(solution)/shard_map/ppermute | solution.py:557
  23.5 0.4 shard_map.93
  23.9 0.1 collective-permute-start.7
  23.9 3.9 %collective-permute-start.8 = (f32[4,16,128]{2,1,0:T(8,128)S(1)}, f32[4,16,128]{2,1,0:T(8,128)S(1)}, u32[]{:S(2)}, u32[]{:S(2)}) collective-permute-start(f32[4,16,128]{2,1,0:T(8,128)S(1)} %get-tuple-element.59), channel_id=1, source_target_pairs={{0,30},{2,4},{4,2},{6,8},{8,6},{10,12},{12,10},{14,16},{16,14},{18... | collective-permute-start | bytes 98312 | tf_op jit(solution)/shard_map/ppermute | solution.py:551
  27.8 9.3 %all_to_all.5 = f32[32,1,128]{2,1,0:T(1,128)S(1)} all-to-all(f32[32,1,128]{2,1,0:T(1,128)S(1)} %get-tuple-element.53), channel_id=1, replica_groups=mesh['district'=16,'coarse'=2] {'district','coarse'}, dimensions={0} | all-to-all | bytes 32768 | tf_op jit(solution)/shard_map/all_to_all | solution.py:658
  37.1 0.0 collective-permute-done.7.near_ref
  37.1 0.2 shard_map.94
  37.3 0.0 collective-permute-done.8.far_ref
  37.3 0.8 %shard_map.95 = (f32[4,16,512]{2,1,0:T(8,128)}, f32[4,16,512]{2,1,0:T(8,128)}) custom-call(f32[4,16,512]{2,1,0:T(8,128)S(1)} %get-tuple-element.56.multiplier_ref, f32[4,16,512]{2,1,0:T(8,128)S(1)} %get-tuple-element.57.partial_ref, f32[8,128]{1,0:T(8,128)S(1)} %get-tuple-element.58.factor_ref, f32[4,16,128]{2,1,0:T(8,128)S(1)} %collective-permute-done.8.far_ref, ...), custom_call_target="tpu_custom_call" | custom-call | tf_op jit(solution)/shard_map/pallas_call | solution.py:516
Async XLA Ops:
  1.5 11.3 %collective-permute-start = (f32[4,16,128]{2,1,0:T(8,128)S(1)}, f32[4,16,128]{2,1,0:T(8,128)S(1)}, u32[]{:S(2)}, u32[]{:S(2)}) collective-permute-start(f32[4,16,128]{2,1,0:T(8,128)S(1)} %get-tuple-element.32), channel_id=1, source_target_pairs={{0,2},{2,0},{4,6},{6,4},{8,10},{10,8},{12,14},{14,12},{16,18},{18,... | collective-permute-start | bytes 98312 | tf_op jit(solution)/shard_map/ppermute | solution.py:552
  4.5 8.2 %collective-permute-start.1 = (f32[4,16,128]{2,1,0:T(8,128)S(1)}, f32[4,16,128]{2,1,0:T(8,128)S(1)}, u32[]{:S(2)}, u32[]{:S(2)}) collective-permute-start(f32[4,16,128]{2,1,0:T(8,128)S(1)} %get-tuple-element.33), channel_id=1, source_target_pairs={{0,30},{2,4},{4,2},{6,8},{8,6},{10,12},{12,10},{14,16},{16,14},{18... | collective-permute-start | bytes 98312 | tf_op jit(solution)/shard_map/ppermute | solution.py:551
  9.1 1.4 %collective-permute-start.2 = (s32[4,8]{1,0:T(4,128)}, s32[4,8]{1,0:T(4,128)S(1)}, u32[]{:S(2)}, u32[]{:S(2)}) collective-permute-start(s32[4,8]{1,0:T(4,128)} %owner_hbm.1), channel_id=1, source_target_pairs={{0,1},{1,0},{2,3},{3,2},{4,5},{5,4},{6,7},{7,6},{8,9},{9,8},{10,11... | collective-permute-start | bytes 392 | tf_op jit(solution)/shard_map/ppermute | solution.py:574
  13.0 1.2 %collective-permute-start.3 = (f32[16,64]{1,0:T(8,128)S(1)}, f32[16,64]{1,0:T(8,128)S(1)}, u32[]{:S(2)}, u32[]{:S(2)}) collective-permute-start(f32[16,64]{1,0:T(8,128)S(1)} %get-tuple-element.42.own_ref), channel_id=1, source_target_pairs={{0,1},{1,0},{2,3},{3,2},{4,5},{5,4},{6,7},{7,6},{8,9},{9,8},{10,11... | collective-permute-start | bytes 12296 | tf_op jit(solution)/shard_map/ppermute | solution.py:557
  14.4 4.0 %collective-permute-start.4 = (f32[4,16,128]{2,1,0:T(8,128)S(1)}, f32[4,16,128]{2,1,0:T(8,128)S(1)}, u32[]{:S(2)}, u32[]{:S(2)}) collective-permute-start(f32[4,16,128]{2,1,0:T(8,128)S(1)} %get-tuple-element.45), channel_id=1, source_target_pairs={{0,2},{2,0},{4,6},{6,4},{8,10},{10,8},{12,14},{14,12},{16,18},{18,... | collective-permute-start | bytes 98312 | tf_op jit(solution)/shard_map/ppermute | solution.py:552
  14.5 7.6 %collective-permute-start.5 = (f32[4,16,128]{2,1,0:T(8,128)S(1)}, f32[4,16,128]{2,1,0:T(8,128)S(1)}, u32[]{:S(2)}, u32[]{:S(2)}) collective-permute-start(f32[4,16,128]{2,1,0:T(8,128)S(1)} %get-tuple-element.46), channel_id=1, source_target_pairs={{0,30},{2,4},{4,2},{6,8},{8,6},{10,12},{12,10},{14,16},{16,14},{18... | collective-permute-start | bytes 98312 | tf_op jit(solution)/shard_map/ppermute | solution.py:551
  22.3 1.2 %collective-permute-start.6 = (f32[16,64]{1,0:T(8,128)S(1)}, f32[16,64]{1,0:T(8,128)S(1)}, u32[]{:S(2)}, u32[]{:S(2)}) collective-permute-start(f32[16,64]{1,0:T(8,128)S(1)} %get-tuple-element.49.own_ref), channel_id=1, source_target_pairs={{0,1},{1,0},{2,3},{3,2},{4,5},{5,4},{6,7},{7,6},{8,9},{9,8},{10,11... | collective-permute-start | bytes 12296 | tf_op jit(solution)/shard_map/ppermute | solution.py:557
  23.9 13.2 %collective-permute-start.7 = (f32[4,16,128]{2,1,0:T(8,128)S(1)}, f32[4,16,128]{2,1,0:T(8,128)S(1)}, u32[]{:S(2)}, u32[]{:S(2)}) collective-permute-start(f32[4,16,128]{2,1,0:T(8,128)S(1)} %get-tuple-element.55), channel_id=1, source_target_pairs={{0,2},{2,0},{4,6},{6,4},{8,10},{10,8},{12,14},{14,12},{16,18},{18,... | collective-permute-start | bytes 98312 | tf_op jit(solution)/shard_map/ppermute | solution.py:552
  23.9 13.4 %collective-permute-start.8 = (f32[4,16,128]{2,1,0:T(8,128)S(1)}, f32[4,16,128]{2,1,0:T(8,128)S(1)}, u32[]{:S(2)}, u32[]{:S(2)}) collective-permute-start(f32[4,16,128]{2,1,0:T(8,128)S(1)} %get-tuple-element.59), channel_id=1, source_target_pairs={{0,30},{2,4},{4,2},{6,8},{8,6},{10,12},{12,10},{14,16},{16,14},{18... | collective-permute-start | bytes 98312 | tf_op jit(solution)/shard_map/ppermute | solution.py:551

commit v3 on v2

--- a/solution.py
+++ b/solution.py
@@ -250,14 +250,17 @@
             yield slot, block, value
 
 
-def corner_sums(dims, high_parts, low_parts, modes_ref):
-    stacked = jnp.concatenate(
-        [jnp.concatenate(high_parts, axis=1), jnp.concatenate(low_parts, axis=1)], axis=0
-    )
+def corner_sums(dims, parts, modes_ref):
+    stacked = jnp.concatenate([jnp.concatenate(part, axis=1) for part in parts], axis=0)
     sums = lax.dot_general(
         stacked, modes_ref[...], (((1,), (1,)), ((), ())), preferred_element_type=F32
     )
-    return sums[: dims.scen] + sums[dims.scen :]
+    return folded(dims, sums)
+
+
+def folded(dims, rows):
+    groups = [rows[i : i + dims.scen] for i in range(0, rows.shape[0], dims.scen)]
+    return functools.reduce(jnp.add, groups)
 
 
 def jump_kernel(
@@ -270,25 +273,22 @@
     modes_ref,
     jump_ref,
     corner_ref,
-):
-    high_parts, low_parts = [], []
+    pieces,
+):
+    parts = [[] for _ in range(pieces)]
     for slot, block, value in jump_blocks(
         dims, field_ref, (near_ref, far_ref), take_ref, weight_ref
     ):
         jump_ref[slot, :, block * LANES : (block + 1) * LANES] = value
-        high, low = halves(value)
-        high_parts.append(high)
-        low_parts.append(low)
-    corner_ref[...] = corner_sums(dims, high_parts, low_parts, modes_ref)
-
-
-def local_term(dims, direction_ref, flex_ref):
-    for slot in range(dims.slots):
-        high, low = halves(direction_ref[slot])
-        both = jnp.dot(
-            jnp.concatenate([high, low], axis=0), flex_ref[slot], preferred_element_type=F32
-        )
-        yield both[: dims.scen] + both[dims.scen :]
+        for part, piece in zip(parts, halves(value)):
+            part.append(piece)
+    corner_ref[...] = corner_sums(dims, parts, modes_ref)
+
+
+def local_term(dims, pieces, direction_ref, flex_ref):
+    for slot in range(dims.slots):
+        forces = jnp.concatenate(halves(direction_ref[slot])[:pieces], axis=0)
+        yield folded(dims, jnp.dot(forces, flex_ref[slot], preferred_element_type=F32))
 
 
 def corner_weights(dims, field_ref, weight_ref, high_ref, low_ref):
@@ -309,7 +309,7 @@
 
 
 def local_kernel(dims, direction_ref, flex_ref, weight_ref, high_ref, low_ref, out_ref, g_ref):
-    for slot, term in enumerate(local_term(dims, direction_ref, flex_ref)):
+    for slot, term in enumerate(local_term(dims, 1, direction_ref, flex_ref)):
         out_ref[slot] = term
     g_ref[...] = corner_weights(dims, direction_ref, weight_ref, high_ref, low_ref)
 
@@ -327,7 +327,7 @@
     sums_ref,
 ):
     acc = [jnp.zeros((dims.scen, LANES), F32)] * 5
-    for slot, term in enumerate(local_term(dims, direction_ref, flex_ref)):
+    for slot, term in enumerate(local_term(dims, 2, direction_ref, flex_ref)):
         out_ref[slot] = term
         for block in range(dims.blocks):
             rhs = block_of(rhs_ref, slot, block)
@@ -612,16 +612,16 @@
         cost=pl.CostEstimate(flops=10**7, bytes_accessed=4 * 10**6, transcendentals=0),
     )
 
-    def jump(field, near, far):
+    def jump(field, near, far, pieces):
         return call(
-            jump_kernel,
+            functools.partial(jump_kernel, pieces=pieces),
             dims,
             (whole, shape((dims.scen, corner_rows), F32)),
             (field, near, far, take, weight, modes),
         )
 
     matmul_cost = pl.CostEstimate(flops=10**8, bytes_accessed=3 * 10**6, transcendentals=0)
-    rhs, part = jump(field, near, far)
+    rhs, part = jump(field, near, far, 1)
     other = from_group(part)
     corners = shape((dims.scen, corner_rows), F32)
     term, rhs_g = call(
@@ -638,7 +638,7 @@
         (term, part, other, high, low, give),
     )
     near, far = exchange(near, far)
-    image, part = jump(response, near, far)
+    image, part = jump(response, near, far, 2)
     other = from_group(part)
     term, image_g, early = call(
         local_last_kernel,

time: 38.3 us -> 38.3 us (level)
  no operation moved by 1% of the time
where the time goes in v3:
time: 38.3 us; the launch traced here: 38.1 us
  starting transfers between devices  15.6 us (41%)
  blocking collectives  9.29 us (24%)
  Pallas kernels  6.35 us (17%)
  waiting for transfers between devices  6.08 us (16%)
  between operations  0.72 us (2%)
    ppermute x3, starting transfers between devices, exchange(): far = lax.ppermute(far, 'district', far_pairs)  12.3 us
    all_to_all x1, blocking collectives, local(): sums = lax.all_to_all(sums, AXES, 0, 0)  9.29 us
    pallas_call x10, Pallas kernels, call(): pl.pallas_call(functools.partial(kernel, dims), out_shape=outs, in_specs=...  6.35 us
    ppermute x3, waiting for transfers between devices, exchange(): far = lax.ppermute(far, 'district', far_pairs)  3.68 us
    ppermute x3, starting transfers between devices, exchange(): near = lax.ppermute(near, 'district', near_pairs)  3.17 us
    ppermute x1, waiting for transfers between devices, local(): others = lax.ppermute(corner_owner, 'coarse', [(0, 1), (1, 0)])  1.37 us
    ppermute x2, waiting for transfers between devices, from_group(): return lax.ppermute(value, 'coarse', [(0, 1), (1, 0)])  0.99 us
  transfers between devices with their start and end apart: 9, of which 4 were waited for; matrix products, arithmetic and copies ran while one was open for 0% of the time, Pallas kernels for 10%

profile of v3, /device:TPU:0, one launch (start us, length us, event | category | flops | bytes accessed | tf_op | source)
XLA Modules:
  0.0 38.1 jit_solution(11334863443182767403)
XLA Ops:
  0.6 0.9 %shard_map.86 = (f32[4,16,128]{2,1,0:T(8,128)S(1)}, f32[4,16,128]{2,1,0:T(8,128)S(1)}, f32[4,16,512]{2,1,0:T(8,128)S(1)}) custom-call(s32[4,4]{1,0:T(4,128)} %partner_hbm.3, f32[4,16,512]{2,1,0:T(8,128)} %free_hbm.1), custom_call_target="tpu_custom_call" | custom-call | tf_op jit(solution)/shard_map/pallas_call | solution.py:516
  1.5 3.0 %collective-permute-start = (f32[4,16,128]{2,1,0:T(8,128)S(1)}, f32[4,16,128]{2,1,0:T(8,128)S(1)}, u32[]{:S(2)}, u32[]{:S(2)}) collective-permute-start(f32[4,16,128]{2,1,0:T(8,128)S(1)} %get-tuple-element.32), channel_id=1, source_target_pairs={{0,2},{2,0},{4,6},{6,4},{8,10},{10,8},{12,14},{14,12},{16,18},{18,... | collective-permute-start | bytes 98312 | tf_op jit(solution)/shard_map/ppermute | solution.py:552
  4.5 4.5 %collective-permute-start.1 = (f32[4,16,128]{2,1,0:T(8,128)S(1)}, f32[4,16,128]{2,1,0:T(8,128)S(1)}, u32[]{:S(2)}, u32[]{:S(2)}) collective-permute-start(f32[4,16,128]{2,1,0:T(8,128)S(1)} %get-tuple-element.33), channel_id=1, source_target_pairs={{0,30},{2,4},{4,2},{6,8},{8,6},{10,12},{12,10},{14,16},{16,14},{18... | collective-permute-start | bytes 98312 | tf_op jit(solution)/shard_map/ppermute | solution.py:551
  9.1 0.0 collective-permute-start.2
  9.1 1.4 %collective-permute-done.2.others_in = s32[4,8]{1,0:T(4,128)S(1)} collective-permute-done((s32[4,8]{1,0:T(4,128)}, s32[4,8]{1,0:T(4,128)S(1)}, u32[]{:S(2)}, u32[]{:S(2)}) %collective-permute-start.2) | collective-permute-done | bytes 160 | tf_op jit(solution)/shard_map/ppermute | solution.py:574
  10.4 2.3 %shard_map.87 = (f32[16,8,128]{2,1,0:T(8,128)S(1)}, f32[16,8,128]{2,1,0:T(8,128)S(1)}, f32[16,8,128]{2,1,0:T(8,128)S(1)}, bf16[64,2048]{1,0:T(8,128)(2,1)S(1)}, ...) custom-call(s32[4,4]{1,0:T(4,128)} %partner_hbm.3, s32[4]{0:T(128)} %iface_hbm.1, ...), custom_call_target="tpu_custom_call" | custom-call | flops 10000000 | bytes 4000000 | tf_op jit(solution)/shard_map/pallas_call | solution.py:516
  12.8 0.0 collective-permute-done.near_ref
  12.8 0.0 collective-permute-done.1.far_ref
  12.8 0.2 shard_map.88
  13.0 0.2 collective-permute-start.3
  13.2 0.5 %shard_map.89 = (f32[4,16,512]{2,1,0:T(8,128)S(1)}, f32[16,64]{1,0:T(8,128)S(1)}) custom-call(f32[4,16,512]{2,1,0:T(8,128)S(1)} %get-tuple-element.37.direction_ref.rhs_ref, bf16[4,512,512]{2,1,0:T(8,128)(2,1)S(1)} %get-tuple-element.38.flex_ref, f32[16,8,128]{2,1,0:T(8,128)S(1)} %get-tuple-element.35.weight_ref, ...), custom_call_target="tpu_custom_call" | custom-call | flops 100000000 | bytes 3000000 | tf_op jit(solution)/shard_map/pallas_call | solution.py:516
  13.7 0.5 %collective-permute-done.3.other_ref = f32[16,64]{1,0:T(8,128)S(1)} collective-permute-done((f32[16,64]{1,0:T(8,128)S(1)}, f32[16,64]{1,0:T(8,128)S(1)}, u32[]{:S(2)}, u32[]{:S(2)}) %collective-permute-start.3) | collective-permute-done | bytes 4128 | tf_op jit(solution)/shard_map/ppermute | solution.py:557
  14.2 0.2 shard_map.90
  14.4 0.1 collective-permute-start.4
  14.5 3.9 %collective-permute-start.5 = (f32[4,16,128]{2,1,0:T(8,128)S(1)}, f32[4,16,128]{2,1,0:T(8,128)S(1)}, u32[]{:S(2)}, u32[]{:S(2)}) collective-permute-start(f32[4,16,128]{2,1,0:T(8,128)S(1)} %get-tuple-element.46), channel_id=1, source_target_pairs={{0,30},{2,4},{4,2},{6,8},{8,6},{10,12},{12,10},{14,16},{16,14},{18... | collective-permute-start | bytes 98312 | tf_op jit(solution)/shard_map/ppermute | solution.py:551
  18.4 0.0 collective-permute-done.4.near_ref
  18.4 3.7 %collective-permute-done.5.far_ref = f32[4,16,128]{2,1,0:T(8,128)S(1)} collective-permute-done((f32[4,16,128]{2,1,0:T(8,128)S(1)}, f32[4,16,128]{2,1,0:T(8,128)S(1)}, u32[]{:S(2)}, u32[]{:S(2)}) %collective-permute-start.5) | collective-permute-done | bytes 32800 | tf_op jit(solution)/shard_map/ppermute | solution.py:551
  22.1 0.2 shard_map.91
  22.3 0.0 collective-permute-start.6
  22.3 0.7 %shard_map.92 = (f32[4,16,512]{2,1,0:T(8,128)S(1)}, f32[16,64]{1,0:T(8,128)S(1)}, f32[1,128]{1,0:T(1,128)S(1)}) custom-call(f32[4,16,512]{2,1,0:T(8,128)S(1)} %get-tuple-element.47.direction_ref.image_ref, bf16[4,512,512]{2,1,0:T(8,128)(2,1)S(1)} %get-tuple-element.38.flex_ref, f32[16,8,128]{2,1,0:T(8,128)S(1)} %get-tuple-element.35.weight_ref, ...), custom_call_target="tpu_custom_call" | custom-call | flops 100000000 | bytes 3000000 | tf_op jit(solution)/shard_map/pallas_call | solution.py:516
  23.0 0.5 %collective-permute-done.6.other_ref = f32[16,64]{1,0:T(8,128)S(1)} collective-permute-done((f32[16,64]{1,0:T(8,128)S(1)}, f32[16,64]{1,0:T(8,128)S(1)}, u32[]{:S(2)}, u32[]{:S(2)}) %collective-permute-start.6) | collective-permute-done | bytes 4128 | tf_op jit(solution)/shard_map/ppermute | solution.py:557
  23.5 0.4 shard_map.93
  23.8 0.1 collective-permute-start.7
  23.9 3.9 %collective-permute-start.8 = (f32[4,16,128]{2,1,0:T(8,128)S(1)}, f32[4,16,128]{2,1,0:T(8,128)S(1)}, u32[]{:S(2)}, u32[]{:S(2)}) collective-permute-start(f32[4,16,128]{2,1,0:T(8,128)S(1)} %get-tuple-element.59), channel_id=1, source_target_pairs={{0,30},{2,4},{4,2},{6,8},{8,6},{10,12},{12,10},{14,16},{16,14},{18... | collective-permute-start | bytes 98312 | tf_op jit(solution)/shard_map/ppermute | solution.py:551
  27.8 9.3 %all_to_all.5 = f32[32,1,128]{2,1,0:T(1,128)S(1)} all-to-all(f32[32,1,128]{2,1,0:T(1,128)S(1)} %get-tuple-element.53), channel_id=1, replica_groups=mesh['district'=16,'coarse'=2] {'district','coarse'}, dimensions={0} | all-to-all | bytes 32768 | tf_op jit(solution)/shard_map/all_to_all | solution.py:658
  37.1 0.0 collective-permute-done.7.near_ref
  37.1 0.2 shard_map.94
  37.3 0.0 collective-permute-done.8.far_ref
  37.3 0.8 %shard_map.95 = (f32[4,16,512]{2,1,0:T(8,128)}, f32[4,16,512]{2,1,0:T(8,128)}) custom-call(f32[4,16,512]{2,1,0:T(8,128)S(1)} %get-tuple-element.56.multiplier_ref, f32[4,16,512]{2,1,0:T(8,128)S(1)} %get-tuple-element.57.partial_ref, f32[8,128]{1,0:T(8,128)S(1)} %get-tuple-element.58.factor_ref, f32[4,16,128]{2,1,0:T(8,128)S(1)} %collective-permute-done.8.far_ref, ...), custom_call_target="tpu_custom_call" | custom-call | tf_op jit(solution)/shard_map/pallas_call | solution.py:516
Async XLA Ops:
  1.5 11.3 %collective-permute-start = (f32[4,16,128]{2,1,0:T(8,128)S(1)}, f32[4,16,128]{2,1,0:T(8,128)S(1)}, u32[]{:S(2)}, u32[]{:S(2)}) collective-permute-start(f32[4,16,128]{2,1,0:T(8,128)S(1)} %get-tuple-element.32), channel_id=1, source_target_pairs={{0,2},{2,0},{4,6},{6,4},{8,10},{10,8},{12,14},{14,12},{16,18},{18,... | collective-permute-start | bytes 98312 | tf_op jit(solution)/shard_map/ppermute | solution.py:552
  4.5 8.2 %collective-permute-start.1 = (f32[4,16,128]{2,1,0:T(8,128)S(1)}, f32[4,16,128]{2,1,0:T(8,128)S(1)}, u32[]{:S(2)}, u32[]{:S(2)}) collective-permute-start(f32[4,16,128]{2,1,0:T(8,128)S(1)} %get-tuple-element.33), channel_id=1, source_target_pairs={{0,30},{2,4},{4,2},{6,8},{8,6},{10,12},{12,10},{14,16},{16,14},{18... | collective-permute-start | bytes 98312 | tf_op jit(solution)/shard_map/ppermute | solution.py:551
  9.1 1.4 %collective-permute-start.2 = (s32[4,8]{1,0:T(4,128)}, s32[4,8]{1,0:T(4,128)S(1)}, u32[]{:S(2)}, u32[]{:S(2)}) collective-permute-start(s32[4,8]{1,0:T(4,128)} %owner_hbm.1), channel_id=1, source_target_pairs={{0,1},{1,0},{2,3},{3,2},{4,5},{5,4},{6,7},{7,6},{8,9},{9,8},{10,11... | collective-permute-start | bytes 392 | tf_op jit(solution)/shard_map/ppermute | solution.py:574
  13.0 1.2 %collective-permute-start.3 = (f32[16,64]{1,0:T(8,128)S(1)}, f32[16,64]{1,0:T(8,128)S(1)}, u32[]{:S(2)}, u32[]{:S(2)}) collective-permute-start(f32[16,64]{1,0:T(8,128)S(1)} %get-tuple-element.42.own_ref), channel_id=1, source_target_pairs={{0,1},{1,0},{2,3},{3,2},{4,5},{5,4},{6,7},{7,6},{8,9},{9,8},{10,11... | collective-permute-start | bytes 12296 | tf_op jit(solution)/shard_map/ppermute | solution.py:557
  14.4 4.0 %collective-permute-start.4 = (f32[4,16,128]{2,1,0:T(8,128)S(1)}, f32[4,16,128]{2,1,0:T(8,128)S(1)}, u32[]{:S(2)}, u32[]{:S(2)}) collective-permute-start(f32[4,16,128]{2,1,0:T(8,128)S(1)} %get-tuple-element.45), channel_id=1, source_target_pairs={{0,2},{2,0},{4,6},{6,4},{8,10},{10,8},{12,14},{14,12},{16,18},{18,... | collective-permute-start | bytes 98312 | tf_op jit(solution)/shard_map/ppermute | solution.py:552
  14.5 7.6 %collective-permute-start.5 = (f32[4,16,128]{2,1,0:T(8,128)S(1)}, f32[4,16,128]{2,1,0:T(8,128)S(1)}, u32[]{:S(2)}, u32[]{:S(2)}) collective-permute-start(f32[4,16,128]{2,1,0:T(8,128)S(1)} %get-tuple-element.46), channel_id=1, source_target_pairs={{0,30},{2,4},{4,2},{6,8},{8,6},{10,12},{12,10},{14,16},{16,14},{18... | collective-permute-start | bytes 98312 | tf_op jit(solution)/shard_map/ppermute | solution.py:551
  22.3 1.2 %collective-permute-start.6 = (f32[16,64]{1,0:T(8,128)S(1)}, f32[16,64]{1,0:T(8,128)S(1)}, u32[]{:S(2)}, u32[]{:S(2)}) collective-permute-start(f32[16,64]{1,0:T(8,128)S(1)} %get-tuple-element.49.own_ref), channel_id=1, source_target_pairs={{0,1},{1,0},{2,3},{3,2},{4,5},{5,4},{6,7},{7,6},{8,9},{9,8},{10,11... | collective-permute-start | bytes 12296 | tf_op jit(solution)/shard_map/ppermute | solution.py:557
  23.8 13.2 %collective-permute-start.7 = (f32[4,16,128]{2,1,0:T(8,128)S(1)}, f32[4,16,128]{2,1,0:T(8,128)S(1)}, u32[]{:S(2)}, u32[]{:S(2)}) collective-permute-start(f32[4,16,128]{2,1,0:T(8,128)S(1)} %get-tuple-element.55), channel_id=1, source_target_pairs={{0,2},{2,0},{4,6},{6,4},{8,10},{10,8},{12,14},{14,12},{16,18},{18,... | collective-permute-start | bytes 98312 | tf_op jit(solution)/shard_map/ppermute | solution.py:552
  23.9 13.4 %collective-permute-start.8 = (f32[4,16,128]{2,1,0:T(8,128)S(1)}, f32[4,16,128]{2,1,0:T(8,128)S(1)}, u32[]{:S(2)}, u32[]{:S(2)}) collective-permute-start(f32[4,16,128]{2,1,0:T(8,128)S(1)} %get-tuple-element.59), channel_id=1, source_target_pairs={{0,30},{2,4},{4,2},{6,8},{8,6},{10,12},{12,10},{14,16},{16,14},{18... | collective-permute-start | bytes 98312 | tf_op jit(solution)/shard_map/ppermute | solution.py:551

commit v4 on v3

--- a/solution.py
+++ b/solution.py
@@ -238,15 +238,22 @@
     return jnp.sum(value, axis=0, keepdims=True)
 
 
+def row_at(ref, place, row):
+    return ref[place, pl.ds(row, 1), :]
+
+
+def left_rows():
+    return jnp.where(remainder(lax.axis_index("district"), 2) == 0, SIDE, 0)
+
+
 def jump_blocks(dims, field_ref, sides, take_ref, weight_ref):
     for slot in range(dims.slots):
         for block in range(dims.blocks):
             place = slot * dims.blocks + block
             value = block_of(field_ref, slot, block) * weight_ref[place, 0:1, :]
-            for side, ref in enumerate(sides):
+            for first, ref in sides:
                 for j in range(SIDE):
-                    row = side * SIDE + j
-                    value = value - take_ref[place, row : row + 1, :] * ref[j]
+                    value = value - row_at(take_ref, place, first + j) * ref[j]
             yield slot, block, value
 
 
@@ -277,7 +284,7 @@
 ):
     parts = [[] for _ in range(pieces)]
     for slot, block, value in jump_blocks(
-        dims, field_ref, (near_ref, far_ref), take_ref, weight_ref
+        dims, field_ref, ((0, near_ref), (SIDE, far_ref)), take_ref, weight_ref
     ):
         jump_ref[slot, :, block * LANES : (block + 1) * LANES] = value
         for part, piece in zip(parts, halves(value)):
@@ -373,15 +380,14 @@
         yield local_ref[slot] + (part[: dims.scen] + part[dims.scen :] + rest)
 
 
-def pack(dims, response, give_ref, near_ref, far_ref):
-    for side, ref in enumerate((near_ref, far_ref)):
+def pack(dims, response, give_ref, sides):
+    for first, ref in sides:
         for j in range(SIDE):
-            row = side * SIDE + j
             value = jnp.zeros((dims.scen, LANES), F32)
             for place in range(dims.per_device):
                 slot, block = divmod(place, dims.blocks)
                 part = response[slot][:, block * LANES : (block + 1) * LANES]
-                value = value + give_ref[place, row : row + 1, :] * part
+                value = value + row_at(give_ref, place, first + j) * part
             ref[j] = value
 
 
@@ -400,7 +406,7 @@
     response = list(add_coarse(dims, local_ref, own_ref[...] + other_ref[...], high_ref, low_ref))
     for slot in range(dims.slots):
         out_ref[slot] = response[slot]
-    pack(dims, response, give_ref, near_ref, far_ref)
+    pack(dims, response, give_ref, ((0, near_ref), (SIDE, far_ref)))
 
 
 def respond_last_kernel(
@@ -415,8 +421,8 @@
     image_g_ref,
     early_ref,
     out_ref,
-    near_ref,
-    far_ref,
+    right_ref,
+    left_ref,
     sums_hbm,
     sums_ref,
     sem,
@@ -429,7 +435,7 @@
     response = list(add_coarse(dims, local_ref, corner, high_ref, low_ref))
     for slot in range(dims.slots):
         out_ref[slot] = response[slot]
-    pack(dims, response, give_ref, near_ref, far_ref)
+    pack(dims, response, give_ref, ((SIDE - left_rows(), right_ref), (left_rows(), left_ref)))
     put.wait()
 
 
@@ -439,7 +445,7 @@
     rhs_ref,
     image_ref,
     field_ref,
-    near_ref,
+    right_ref,
     take_ref,
     weight_ref,
     multiplier_ref,
@@ -458,7 +464,7 @@
     on_second = step_next * step
     factor_ref[...] = jnp.broadcast_to(on_second, factor_ref.shape)
     for slot, block, second_image in jump_blocks(
-        dims, field_ref, (near_ref,), take_ref, weight_ref
+        dims, field_ref, ((SIDE - left_rows(), right_ref),), take_ref, weight_ref
     ):
         lanes = slice(block * LANES, (block + 1) * LANES)
         rhs = rhs_ref[slot, :, lanes]
@@ -472,7 +478,7 @@
     multiplier_ref,
     partial_ref,
     factor_ref,
-    far_ref,
+    left_ref,
     take_ref,
     multiplier_hbm,
     residual_hbm,
@@ -488,14 +494,15 @@
     for put in puts:
         put.start()
     factor = factor_ref[0:1, :]
-    sides = [factor * far_ref[j] for j in range(SIDE)]
+    shares = [factor * left_ref[j] for j in range(SIDE)]
+    first = left_rows()
     for slot in range(dims.slots):
         for block in range(dims.blocks):
             place = slot * dims.blocks + block
             lanes = slice(block * LANES, (block + 1) * LANES)
             value = partial_ref[slot, :, lanes]
             for j in range(SIDE):
-                value = value - take_ref[place, SIDE + j : SIDE + j + 1, :] * sides[j]
+                value = value - row_at(take_ref, place, first + j) * shares[j]
             residual_ref[slot, :, lanes] = value
         put = pltpu.make_async_copy(residual_ref.at[slot], residual_hbm.at[slot], sems.at[1, slot])
         put.start()
@@ -546,6 +553,10 @@
     far_pairs = [
         (d, (d - 1 if d % 2 == 0 else d + 1) % dims.districts) for d in range(dims.districts)
     ]
+
+    def passed_along(value, steps):
+        count = dims.districts
+        return lax.ppermute(value, "district", [(d, (d + steps) % count) for d in range(count)])
 
     def exchange(near, far):
         far = lax.ppermute(far, "district", far_pairs)
@@ -647,7 +658,7 @@
         (image, flex, weight, high, low, rhs),
         cost=matmul_cost,
     )
-    response, near, far, sums = call(
+    response, right, left, sums = call(
         respond_last_kernel,
         dims,
         (whole, packed, packed, shape((devices, 1, LANES), F32)),
@@ -656,18 +667,19 @@
         scratch=[pltpu.VMEM((devices, 1, LANES), F32), pltpu.SemaphoreType.DMA],
     )
     sums = lax.all_to_all(sums, AXES, 0, 0)
-    near, far = exchange(near, far)
+    from_left = passed_along(right, 1)
+    from_right = passed_along(left, -1)
     multiplier, residual, factor = call(
         settle_kernel,
         dims,
         (whole, whole, shape((TILE, LANES), F32)),
-        (sums.reshape(devices, LANES), rhs, image, response, near, take, weight),
+        (sums.reshape(devices, LANES), rhs, image, response, from_right, take, weight),
     )
     return call(
         finish_kernel,
         dims,
         (whole, whole),
-        (multiplier, residual, factor, far, take),
+        (multiplier, residual, factor, from_left, take),
         out_specs=(HBM, HBM),
         scratch=[pltpu.VMEM(free_response.shape, F32), pltpu.SemaphoreType.DMA((2, dims.slots))],
     )

time: 38.3 us -> 41.9 us (1.094)
  blocking collectives: 9.29 us -> 13 us
    ppermute x3 -> x2, starting transfers between devices: 12.3 us -> 8.4 us  [exchange(): far = lax.ppermute(far, 'district', far_pairs)]
    ppermute x0 -> x2, starting transfers between devices: none -> 3.86 us  [passed_along(): lax.ppermute(value, 'district', [(d, (d + steps) % count) for d in range(...]
    all_to_all x1, blocking collectives: 9.29 us -> 13 us  [local(): sums = lax.all_to_all(sums, AXES, 0, 0)]
    ppermute x3 -> x2, starting transfers between devices: 3.17 us -> 3.1 us  [exchange(): near = lax.ppermute(near, 'district', near_pairs)]
    ppermute x3 -> x2, waiting for transfers between devices: 3.68 us -> 3.68 us  [exchange(): far = lax.ppermute(far, 'district', far_pairs)]
  transfers between devices with their start and end apart: 9 -> 9, of which waited for: 4 -> 4; matrix products, arithmetic and copies ran while one was open for 0% -> 0% of each run, Pallas kernels for 10% -> 9%
where the time goes in v4:
time: 41.9 us; the launch traced here: 41.6 us
  starting transfers between devices  15.5 us (37%)
  blocking collectives  13 us (31%)
  Pallas kernels  6.35 us (15%)
  waiting for transfers between devices  6.08 us (15%)
  between operations  0.71 us (2%)
    all_to_all x1, blocking collectives, local(): sums = lax.all_to_all(sums, AXES, 0, 0)  13 us
    ppermute x2, starting transfers between devices, exchange(): far = lax.ppermute(far, 'district', far_pairs)  8.4 us
    pallas_call x10, Pallas kernels, call(): pl.pallas_call(functools.partial(kernel, dims), out_shape=outs, in_specs=...  6.35 us
    ppermute x2, starting transfers between devices, passed_along(): lax.ppermute(value, 'district', [(d, (d + steps) % count) for d in range(...  3.86 us
    ppermute x2, waiting for transfers between devices, exchange(): far = lax.ppermute(far, 'district', far_pairs)  3.68 us
    ppermute x2, starting transfers between devices, exchange(): near = lax.ppermute(near, 'district', near_pairs)  3.1 us
    ppermute x1, waiting for transfers between devices, local(): others = lax.ppermute(corner_owner, 'coarse', [(0, 1), (1, 0)])  1.37 us
    ppermute x2, waiting for transfers between devices, from_group(): return lax.ppermute(value, 'coarse', [(0, 1), (1, 0)])  0.99 us
  transfers between devices with their start and end apart: 9, of which 4 were waited for; matrix products, arithmetic and copies ran while one was open for 0% of the time, Pallas kernels for 9%

profile of v4, /device:TPU:0, one launch (start us, length us, event | category | flops | bytes accessed | tf_op | source)
XLA Modules:
  0.0 41.6 jit_solution(16268157678180764218)
XLA Ops:
  0.6 0.9 %shard_map.86 = (f32[4,16,128]{2,1,0:T(8,128)S(1)}, f32[4,16,128]{2,1,0:T(8,128)S(1)}, f32[4,16,512]{2,1,0:T(8,128)S(1)}) custom-call(s32[4,4]{1,0:T(4,128)} %partner_hbm.3, f32[4,16,512]{2,1,0:T(8,128)} %free_hbm.1), custom_call_target="tpu_custom_call" | custom-call | tf_op jit(solution)/shard_map/pallas_call | solution.py:523
  1.5 3.0 %collective-permute-start = (f32[4,16,128]{2,1,0:T(8,128)S(1)}, f32[4,16,128]{2,1,0:T(8,128)S(1)}, u32[]{:S(2)}, u32[]{:S(2)}) collective-permute-start(f32[4,16,128]{2,1,0:T(8,128)S(1)} %get-tuple-element.32), channel_id=1, source_target_pairs={{0,2},{2,0},{4,6},{6,4},{8,10},{10,8},{12,14},{14,12},{16,18},{18,... | collective-permute-start | bytes 98312 | tf_op jit(solution)/shard_map/ppermute | solution.py:563
  4.5 4.5 %collective-permute-start.1 = (f32[4,16,128]{2,1,0:T(8,128)S(1)}, f32[4,16,128]{2,1,0:T(8,128)S(1)}, u32[]{:S(2)}, u32[]{:S(2)}) collective-permute-start(f32[4,16,128]{2,1,0:T(8,128)S(1)} %get-tuple-element.33), channel_id=1, source_target_pairs={{0,30},{2,4},{4,2},{6,8},{8,6},{10,12},{12,10},{14,16},{16,14},{18... | collective-permute-start | bytes 98312 | tf_op jit(solution)/shard_map/ppermute | solution.py:562
  9.1 0.0 collective-permute-start.2
  9.1 1.4 %collective-permute-done.2.others_in = s32[4,8]{1,0:T(4,128)S(1)} collective-permute-done((s32[4,8]{1,0:T(4,128)}, s32[4,8]{1,0:T(4,128)S(1)}, u32[]{:S(2)}, u32[]{:S(2)}) %collective-permute-start.2) | collective-permute-done | bytes 160 | tf_op jit(solution)/shard_map/ppermute | solution.py:585
  10.4 2.3 %shard_map.87 = (f32[16,8,128]{2,1,0:T(8,128)S(1)}, f32[16,8,128]{2,1,0:T(8,128)S(1)}, f32[16,8,128]{2,1,0:T(8,128)S(1)}, bf16[64,2048]{1,0:T(8,128)(2,1)S(1)}, ...) custom-call(s32[4,4]{1,0:T(4,128)} %partner_hbm.3, s32[4]{0:T(128)} %iface_hbm.1, ...), custom_call_target="tpu_custom_call" | custom-call | flops 10000000 | bytes 4000000 | tf_op jit(solution)/shard_map/pallas_call | solution.py:523
  12.8 0.0 collective-permute-done.near_ref
  12.8 0.0 collective-permute-done.1.far_ref
  12.8 0.2 shard_map.88
  13.0 0.2 collective-permute-start.3
  13.2 0.5 %shard_map.89 = (f32[4,16,512]{2,1,0:T(8,128)S(1)}, f32[16,64]{1,0:T(8,128)S(1)}) custom-call(f32[4,16,512]{2,1,0:T(8,128)S(1)} %get-tuple-element.37.direction_ref.rhs_ref, bf16[4,512,512]{2,1,0:T(8,128)(2,1)S(1)} %get-tuple-element.38.flex_ref, f32[16,8,128]{2,1,0:T(8,128)S(1)} %get-tuple-element.35.weight_ref, ...), custom_call_target="tpu_custom_call" | custom-call | flops 100000000 | bytes 3000000 | tf_op jit(solution)/shard_map/pallas_call | solution.py:523
  13.7 0.5 %collective-permute-done.3.other_ref = f32[16,64]{1,0:T(8,128)S(1)} collective-permute-done((f32[16,64]{1,0:T(8,128)S(1)}, f32[16,64]{1,0:T(8,128)S(1)}, u32[]{:S(2)}, u32[]{:S(2)}) %collective-permute-start.3) | collective-permute-done | bytes 4128 | tf_op jit(solution)/shard_map/ppermute | solution.py:568
  14.2 0.2 shard_map.90
  14.4 0.1 collective-permute-start.4
  14.5 3.9 %collective-permute-start.5 = (f32[4,16,128]{2,1,0:T(8,128)S(1)}, f32[4,16,128]{2,1,0:T(8,128)S(1)}, u32[]{:S(2)}, u32[]{:S(2)}) collective-permute-start(f32[4,16,128]{2,1,0:T(8,128)S(1)} %get-tuple-element.46), channel_id=1, source_target_pairs={{0,30},{2,4},{4,2},{6,8},{8,6},{10,12},{12,10},{14,16},{16,14},{18... | collective-permute-start | bytes 98312 | tf_op jit(solution)/shard_map/ppermute | solution.py:562
  18.4 0.0 collective-permute-done.4.near_ref
  18.4 3.7 %collective-permute-done.5.far_ref = f32[4,16,128]{2,1,0:T(8,128)S(1)} collective-permute-done((f32[4,16,128]{2,1,0:T(8,128)S(1)}, f32[4,16,128]{2,1,0:T(8,128)S(1)}, u32[]{:S(2)}, u32[]{:S(2)}) %collective-permute-start.5) | collective-permute-done | bytes 32800 | tf_op jit(solution)/shard_map/ppermute | solution.py:562
  22.1 0.2 shard_map.91
  22.3 0.0 collective-permute-start.6
  22.3 0.7 %shard_map.92 = (f32[4,16,512]{2,1,0:T(8,128)S(1)}, f32[16,64]{1,0:T(8,128)S(1)}, f32[1,128]{1,0:T(1,128)S(1)}) custom-call(f32[4,16,512]{2,1,0:T(8,128)S(1)} %get-tuple-element.47.direction_ref.image_ref, bf16[4,512,512]{2,1,0:T(8,128)(2,1)S(1)} %get-tuple-element.38.flex_ref, f32[16,8,128]{2,1,0:T(8,128)S(1)} %get-tuple-element.35.weight_ref, ...), custom_call_target="tpu_custom_call" | custom-call | flops 100000000 | bytes 3000000 | tf_op jit(solution)/shard_map/pallas_call | solution.py:523
  23.0 0.5 %collective-permute-done.6.other_ref = f32[16,64]{1,0:T(8,128)S(1)} collective-permute-done((f32[16,64]{1,0:T(8,128)S(1)}, f32[16,64]{1,0:T(8,128)S(1)}, u32[]{:S(2)}, u32[]{:S(2)}) %collective-permute-start.6) | collective-permute-done | bytes 4128 | tf_op jit(solution)/shard_map/ppermute | solution.py:568
  23.5 0.4 shard_map.93
  23.8 3.9 %collective-permute-start.7 = (f32[4,16,128]{2,1,0:T(8,128)S(1)}, f32[4,16,128]{2,1,0:T(8,128)S(1)}, u32[]{:S(2)}, u32[]{:S(2)}) collective-permute-start(f32[4,16,128]{2,1,0:T(8,128)S(1)} %get-tuple-element.55), channel_id=1, source_target_pairs={{0,30},{2,0},{4,2},{6,4},{8,6},{10,8},{12,10},{14,12},{16,14},{18,... | collective-permute-start | bytes 98312 | tf_op jit(solution)/shard_map/ppermute | solution.py:559
  27.7 0.0 collective-permute-start.8
  27.7 13.0 %all_to_all.5 = f32[32,1,128]{2,1,0:T(1,128)S(1)} all-to-all(f32[32,1,128]{2,1,0:T(1,128)S(1)} %get-tuple-element.53), channel_id=1, replica_groups=mesh['district'=16,'coarse'=2] {'district','coarse'}, dimensions={0} | all-to-all | bytes 32768 | tf_op jit(solution)/shard_map/all_to_all | solution.py:669
  40.7 0.0 collective-permute-done.7.right_ref
  40.7 0.2 shard_map.94
  40.9 0.0 collective-permute-done.8.left_ref
  40.9 0.8 %shard_map.95 = (f32[4,16,512]{2,1,0:T(8,128)}, f32[4,16,512]{2,1,0:T(8,128)}) custom-call(f32[4,16,512]{2,1,0:T(8,128)S(1)} %get-tuple-element.56.multiplier_ref, f32[4,16,512]{2,1,0:T(8,128)S(1)} %get-tuple-element.57.partial_ref, f32[8,128]{1,0:T(8,128)S(1)} %get-tuple-element.58.factor_ref, f32[4,16,128]{2,1,0:T(8,128)S(1)} %collective-permute-done.8.left_ref, ...), custom_call_target="tpu_custom_call" | custom-call | tf_op jit(solution)/shard_map/pallas_call | solution.py:523
Async XLA Ops:
  1.5 11.3 %collective-permute-start = (f32[4,16,128]{2,1,0:T(8,128)S(1)}, f32[4,16,128]{2,1,0:T(8,128)S(1)}, u32[]{:S(2)}, u32[]{:S(2)}) collective-permute-start(f32[4,16,128]{2,1,0:T(8,128)S(1)} %get-tuple-element.32), channel_id=1, source_target_pairs={{0,2},{2,0},{4,6},{6,4},{8,10},{10,8},{12,14},{14,12},{16,18},{18,... | collective-permute-start | bytes 98312 | tf_op jit(solution)/shard_map/ppermute | solution.py:563
  4.5 8.2 %collective-permute-start.1 = (f32[4,16,128]{2,1,0:T(8,128)S(1)}, f32[4,16,128]{2,1,0:T(8,128)S(1)}, u32[]{:S(2)}, u32[]{:S(2)}) collective-permute-start(f32[4,16,128]{2,1,0:T(8,128)S(1)} %get-tuple-element.33), channel_id=1, source_target_pairs={{0,30},{2,4},{4,2},{6,8},{8,6},{10,12},{12,10},{14,16},{16,14},{18... | collective-permute-start | bytes 98312 | tf_op jit(solution)/shard_map/ppermute | solution.py:562
  9.1 1.4 %collective-permute-start.2 = (s32[4,8]{1,0:T(4,128)}, s32[4,8]{1,0:T(4,128)S(1)}, u32[]{:S(2)}, u32[]{:S(2)}) collective-permute-start(s32[4,8]{1,0:T(4,128)} %owner_hbm.1), channel_id=1, source_target_pairs={{0,1},{1,0},{2,3},{3,2},{4,5},{5,4},{6,7},{7,6},{8,9},{9,8},{10,11... | collective-permute-start | bytes 392 | tf_op jit(solution)/shard_map/ppermute | solution.py:585
  13.0 1.2 %collective-permute-start.3 = (f32[16,64]{1,0:T(8,128)S(1)}, f32[16,64]{1,0:T(8,128)S(1)}, u32[]{:S(2)}, u32[]{:S(2)}) collective-permute-start(f32[16,64]{1,0:T(8,128)S(1)} %get-tuple-element.42.own_ref), channel_id=1, source_target_pairs={{0,1},{1,0},{2,3},{3,2},{4,5},{5,4},{6,7},{7,6},{8,9},{9,8},{10,11... | collective-permute-start | bytes 12296 | tf_op jit(solution)/shard_map/ppermute | solution.py:568
  14.4 4.0 %collective-permute-start.4 = (f32[4,16,128]{2,1,0:T(8,128)S(1)}, f32[4,16,128]{2,1,0:T(8,128)S(1)}, u32[]{:S(2)}, u32[]{:S(2)}) collective-permute-start(f32[4,16,128]{2,1,0:T(8,128)S(1)} %get-tuple-element.45), channel_id=1, source_target_pairs={{0,2},{2,0},{4,6},{6,4},{8,10},{10,8},{12,14},{14,12},{16,18},{18,... | collective-permute-start | bytes 98312 | tf_op jit(solution)/shard_map/ppermute | solution.py:563
  14.5 7.6 %collective-permute-start.5 = (f32[4,16,128]{2,1,0:T(8,128)S(1)}, f32[4,16,128]{2,1,0:T(8,128)S(1)}, u32[]{:S(2)}, u32[]{:S(2)}) collective-permute-start(f32[4,16,128]{2,1,0:T(8,128)S(1)} %get-tuple-element.46), channel_id=1, source_target_pairs={{0,30},{2,4},{4,2},{6,8},{8,6},{10,12},{12,10},{14,16},{16,14},{18... | collective-permute-start | bytes 98312 | tf_op jit(solution)/shard_map/ppermute | solution.py:562
  22.3 1.2 %collective-permute-start.6 = (f32[16,64]{1,0:T(8,128)S(1)}, f32[16,64]{1,0:T(8,128)S(1)}, u32[]{:S(2)}, u32[]{:S(2)}) collective-permute-start(f32[16,64]{1,0:T(8,128)S(1)} %get-tuple-element.49.own_ref), channel_id=1, source_target_pairs={{0,1},{1,0},{2,3},{3,2},{4,5},{5,4},{6,7},{7,6},{8,9},{9,8},{10,11... | collective-permute-start | bytes 12296 | tf_op jit(solution)/shard_map/ppermute | solution.py:568
  23.8 16.8 %collective-permute-start.7 = (f32[4,16,128]{2,1,0:T(8,128)S(1)}, f32[4,16,128]{2,1,0:T(8,128)S(1)}, u32[]{:S(2)}, u32[]{:S(2)}) collective-permute-start(f32[4,16,128]{2,1,0:T(8,128)S(1)} %get-tuple-element.55), channel_id=1, source_target_pairs={{0,30},{2,0},{4,2},{6,4},{8,6},{10,8},{12,10},{14,12},{16,14},{18,... | collective-permute-start | bytes 98312 | tf_op jit(solution)/shard_map/ppermute | solution.py:559
  27.7 13.2 %collective-permute-start.8 = (f32[4,16,128]{2,1,0:T(8,128)S(1)}, f32[4,16,128]{2,1,0:T(8,128)S(1)}, u32[]{:S(2)}, u32[]{:S(2)}) collective-permute-start(f32[4,16,128]{2,1,0:T(8,128)S(1)} %get-tuple-element.59), channel_id=1, source_target_pairs={{0,2},{2,4},{4,6},{6,8},{8,10},{10,12},{12,14},{14,16},{16,18},{18... | collective-permute-start | bytes 98312 | tf_op jit(solution)/shard_map/ppermute | solution.py:559

commit v5 on v4

--- a/solution.py
+++ b/solution.py
@@ -67,8 +67,12 @@
     return out
 
 
-def block_of(ref, slot, block):
-    return ref[slot, :, block * LANES : (block + 1) * LANES]
+def lanes_of(dims, block):
+    return slice(block * dims.block_width, (block + 1) * dims.block_width)
+
+
+def block_of(dims, ref, slot, block):
+    return ref[slot, :, lanes_of(dims, block)]
 
 
 def pack_first_kernel(
@@ -94,8 +98,9 @@
         fetch.wait()
     for slot in range(2 * SIDE):
         place = order[slot]
-        lane = pl.multiple_of(remainder(place, dims.blocks) * LANES, LANES)
-        value = free_ref[quotient(place, dims.blocks), :, pl.ds(lane, LANES)]
+        lane = remainder(place, dims.blocks) * dims.block_width
+        lanes = pl.ds(pl.multiple_of(lane, dims.block_width), dims.block_width)
+        value = free_ref[quotient(place, dims.blocks), :, lanes]
         if slot < SIDE:
             near_ref[slot] = value
         else:
@@ -144,7 +149,7 @@
     for fetch in fetches[:-1]:
         fetch.wait()
     faces = facing(partner_ref, dims)
-    row = lax.broadcasted_iota(jnp.int32, (TILE, LANES), 0)
+    row = lax.broadcasted_iota(jnp.int32, (TILE, dims.block_width), 0)
     near_count = jnp.int32(0)
     far_count = jnp.int32(0)
     for place, (near, far, whole) in enumerate(faces):
@@ -250,7 +255,7 @@
     for slot in range(dims.slots):
         for block in range(dims.blocks):
             place = slot * dims.blocks + block
-            value = block_of(field_ref, slot, block) * weight_ref[place, 0:1, :]
+            value = block_of(dims, field_ref, slot, block) * weight_ref[place, 0:1, :]
             for first, ref in sides:
                 for j in range(SIDE):
                     value = value - row_at(take_ref, place, first + j) * ref[j]
@@ -286,7 +291,7 @@
     for slot, block, value in jump_blocks(
         dims, field_ref, ((0, near_ref), (SIDE, far_ref)), take_ref, weight_ref
     ):
-        jump_ref[slot, :, block * LANES : (block + 1) * LANES] = value
+        jump_ref[slot, :, lanes_of(dims, block)] = value
         for part, piece in zip(parts, halves(value)):
             part.append(piece)
     corner_ref[...] = corner_sums(dims, parts, modes_ref)
@@ -303,7 +308,7 @@
     for slot in range(dims.slots):
         for block in range(dims.blocks):
             place = slot * dims.blocks + block
-            value = block_of(field_ref, slot, block) * weight_ref[place, 1:2, :]
+            value = block_of(dims, field_ref, slot, block) * weight_ref[place, 1:2, :]
             high, low = halves(value)
             high_parts.append(high)
             low_parts.append(low)
@@ -333,15 +338,15 @@
     g_ref,
     sums_ref,
 ):
-    acc = [jnp.zeros((dims.scen, LANES), F32)] * 5
+    acc = [jnp.zeros((dims.scen, dims.block_width), F32)] * 5
     for slot, term in enumerate(local_term(dims, 2, direction_ref, flex_ref)):
         out_ref[slot] = term
         for block in range(dims.blocks):
-            rhs = block_of(rhs_ref, slot, block)
-            image = block_of(direction_ref, slot, block)
+            rhs = block_of(dims, rhs_ref, slot, block)
+            image = block_of(dims, direction_ref, slot, block)
             doubled = (
                 weight_ref[slot * dims.blocks + block, 1:2, :]
-                * term[:, block * LANES : (block + 1) * LANES]
+                * term[:, lanes_of(dims, block)]
             )
             for q, product in enumerate(
                 (rhs * rhs, rhs * image, image * image, rhs * doubled, image * doubled)
@@ -383,10 +388,10 @@
 def pack(dims, response, give_ref, sides):
     for first, ref in sides:
         for j in range(SIDE):
-            value = jnp.zeros((dims.scen, LANES), F32)
+            value = jnp.zeros((dims.scen, dims.block_width), F32)
             for place in range(dims.per_device):
                 slot, block = divmod(place, dims.blocks)
-                part = response[slot][:, block * LANES : (block + 1) * LANES]
+                part = response[slot][:, lanes_of(dims, block)]
                 value = value + row_at(give_ref, place, first + j) * part
             ref[j] = value
 
@@ -432,10 +437,16 @@
     sums_ref[...] = jnp.broadcast_to((early_ref[...] + late)[None], sums_ref.shape)
     put = pltpu.make_async_copy(sums_ref, sums_hbm, sem)
     put.start()
-    response = list(add_coarse(dims, local_ref, corner, high_ref, low_ref))
-    for slot in range(dims.slots):
-        out_ref[slot] = response[slot]
-    pack(dims, response, give_ref, ((SIDE - left_rows(), right_ref), (left_rows(), left_ref)))
+
+    @pl.when(lax.axis_index("district") >= 0)
+    def _():
+        sums = own_ref[...] + other_ref[...]
+        response = list(add_coarse(dims, local_ref, sums, high_ref, low_ref))
+        for slot in range(dims.slots):
+            out_ref[slot] = response[slot]
+        sides = ((SIDE - left_rows(), right_ref), (left_rows(), left_ref))
+        pack(dims, response, give_ref, sides)
+
     put.wait()
 
 
@@ -466,7 +477,7 @@
     for slot, block, second_image in jump_blocks(
         dims, field_ref, ((SIDE - left_rows(), right_ref),), take_ref, weight_ref
     ):
-        lanes = slice(block * LANES, (block + 1) * LANES)
+        lanes = lanes_of(dims, block)
         rhs = rhs_ref[slot, :, lanes]
         image = image_ref[slot, :, lanes]
         multiplier_ref[slot, :, lanes] = on_first * rhs - on_second * image
@@ -499,7 +510,7 @@
     for slot in range(dims.slots):
         for block in range(dims.blocks):
             place = slot * dims.blocks + block
-            lanes = slice(block * LANES, (block + 1) * LANES)
+            lanes = lanes_of(dims, block)
             value = partial_ref[slot, :, lanes]
             for j in range(SIDE):
                 value = value - row_at(take_ref, place, first + j) * shares[j]
@@ -537,6 +548,7 @@
     dims = Dims()
     dims.slots, dims.scen, dims.width = free_response.shape
     dims.blocks = partner.shape[1]
+    dims.block_width = dims.width // dims.blocks
     dims.per_device = dims.slots * dims.blocks
     dims.coarse_width = coarse_inverse.shape[1]
     dims.corners = corner_modes.shape[1]
@@ -545,8 +557,8 @@
     devices = dims.districts * dims.coarse
     shape = jax.ShapeDtypeStruct
     whole = shape(free_response.shape, F32)
-    packed = shape((SIDE, dims.scen, LANES), F32)
-    per_block = shape((dims.per_device, TILE, LANES), F32)
+    packed = shape((SIDE, dims.scen, dims.block_width), F32)
+    per_block = shape((dims.per_device, TILE, dims.block_width), F32)
     corner_rows = dims.slots * dims.corners * dims.coarse
 
     near_pairs = [(d, d + 1 if d % 2 == 0 else d - 1) for d in range(dims.districts)]
@@ -672,7 +684,7 @@
     multiplier, residual, factor = call(
         settle_kernel,
         dims,
-        (whole, whole, shape((TILE, LANES), F32)),
+        (whole, whole, shape((TILE, dims.block_width), F32)),
         (sums.reshape(devices, LANES), rhs, image, response, from_right, take, weight),
     )
     return call(

time: 41.9 us -> 41.9 us (level)
  no operation moved by 1% of the time
where the time goes in v5:
time: 41.9 us; the launch traced here: 41.6 us
  starting transfers between devices  15.5 us (37%)
  blocking collectives  13 us (31%)
  Pallas kernels  6.36 us (15%)
  waiting for transfers between devices  6.08 us (15%)
  between operations  0.71 us (2%)
    all_to_all x1, blocking collectives, local(): sums = lax.all_to_all(sums, AXES, 0, 0)  13 us
    ppermute x2, starting transfers between devices, exchange(): far = lax.ppermute(far, 'district', far_pairs)  8.4 us
    pallas_call x10, Pallas kernels, call(): pl.pallas_call(functools.partial(kernel, dims), out_shape=outs, in_specs=...  6.36 us
    ppermute x2, starting transfers between devices, passed_along(): lax.ppermute(value, 'district', [(d, (d + steps) % count) for d in range(...  3.86 us
    ppermute x2, waiting for transfers between devices, exchange(): far = lax.ppermute(far, 'district', far_pairs)  3.68 us
    ppermute x2, starting transfers between devices, exchange(): near = lax.ppermute(near, 'district', near_pairs)  3.1 us
    ppermute x1, waiting for transfers between devices, local(): others = lax.ppermute(corner_owner, 'coarse', [(0, 1), (1, 0)])  1.37 us
    ppermute x2, waiting for transfers between devices, from_group(): return lax.ppermute(value, 'coarse', [(0, 1), (1, 0)])  0.99 us
  transfers between devices with their start and end apart: 9, of which 4 were waited for; matrix products, arithmetic and copies ran while one was open for 0% of the time, Pallas kernels for 9%

profile of v5, /device:TPU:0, one launch (start us, length us, event | category | flops | bytes accessed | tf_op | source)
XLA Modules:
  0.0 41.6 jit_solution(9497666163853851913)
XLA Ops:
  0.6 0.9 %shard_map.86 = (f32[4,16,128]{2,1,0:T(8,128)S(1)}, f32[4,16,128]{2,1,0:T(8,128)S(1)}, f32[4,16,512]{2,1,0:T(8,128)S(1)}) custom-call(s32[4,4]{1,0:T(4,128)} %partner_hbm.3, f32[4,16,512]{2,1,0:T(8,128)} %free_hbm.1), custom_call_target="tpu_custom_call" | custom-call | tf_op jit(solution)/shard_map/pallas_call | solution.py:534
  1.5 3.0 %collective-permute-start = (f32[4,16,128]{2,1,0:T(8,128)S(1)}, f32[4,16,128]{2,1,0:T(8,128)S(1)}, u32[]{:S(2)}, u32[]{:S(2)}) collective-permute-start(f32[4,16,128]{2,1,0:T(8,128)S(1)} %get-tuple-element.32), channel_id=1, source_target_pairs={{0,2},{2,0},{4,6},{6,4},{8,10},{10,8},{12,14},{14,12},{16,18},{18,... | collective-permute-start | bytes 98312 | tf_op jit(solution)/shard_map/ppermute | solution.py:575
  4.5 4.5 %collective-permute-start.1 = (f32[4,16,128]{2,1,0:T(8,128)S(1)}, f32[4,16,128]{2,1,0:T(8,128)S(1)}, u32[]{:S(2)}, u32[]{:S(2)}) collective-permute-start(f32[4,16,128]{2,1,0:T(8,128)S(1)} %get-tuple-element.33), channel_id=1, source_target_pairs={{0,30},{2,4},{4,2},{6,8},{8,6},{10,12},{12,10},{14,16},{16,14},{18... | collective-permute-start | bytes 98312 | tf_op jit(solution)/shard_map/ppermute | solution.py:574
  9.1 0.0 collective-permute-start.2
  9.1 1.4 %collective-permute-done.2.others_in = s32[4,8]{1,0:T(4,128)S(1)} collective-permute-done((s32[4,8]{1,0:T(4,128)}, s32[4,8]{1,0:T(4,128)S(1)}, u32[]{:S(2)}, u32[]{:S(2)}) %collective-permute-start.2) | collective-permute-done | bytes 160 | tf_op jit(solution)/shard_map/ppermute | solution.py:597
  10.4 2.3 %shard_map.87 = (f32[16,8,128]{2,1,0:T(8,128)S(1)}, f32[16,8,128]{2,1,0:T(8,128)S(1)}, f32[16,8,128]{2,1,0:T(8,128)S(1)}, bf16[64,2048]{1,0:T(8,128)(2,1)S(1)}, ...) custom-call(s32[4,4]{1,0:T(4,128)} %partner_hbm.3, s32[4]{0:T(128)} %iface_hbm.1, ...), custom_call_target="tpu_custom_call" | custom-call | flops 10000000 | bytes 4000000 | tf_op jit(solution)/shard_map/pallas_call | solution.py:534
  12.8 0.0 collective-permute-done.near_ref
  12.8 0.0 collective-permute-done.1.far_ref
  12.8 0.2 shard_map.88
  13.0 0.2 collective-permute-start.3
  13.2 0.5 %shard_map.89 = (f32[4,16,512]{2,1,0:T(8,128)S(1)}, f32[16,64]{1,0:T(8,128)S(1)}) custom-call(f32[4,16,512]{2,1,0:T(8,128)S(1)} %get-tuple-element.37.direction_ref.rhs_ref, bf16[4,512,512]{2,1,0:T(8,128)(2,1)S(1)} %get-tuple-element.38.flex_ref, f32[16,8,128]{2,1,0:T(8,128)S(1)} %get-tuple-element.35.weight_ref, ...), custom_call_target="tpu_custom_call" | custom-call | flops 100000000 | bytes 3000000 | tf_op jit(solution)/shard_map/pallas_call | solution.py:534
  13.7 0.5 %collective-permute-done.3.other_ref = f32[16,64]{1,0:T(8,128)S(1)} collective-permute-done((f32[16,64]{1,0:T(8,128)S(1)}, f32[16,64]{1,0:T(8,128)S(1)}, u32[]{:S(2)}, u32[]{:S(2)}) %collective-permute-start.3) | collective-permute-done | bytes 4128 | tf_op jit(solution)/shard_map/ppermute | solution.py:580
  14.2 0.2 shard_map.90
  14.4 0.1 collective-permute-start.4
  14.5 3.9 %collective-permute-start.5 = (f32[4,16,128]{2,1,0:T(8,128)S(1)}, f32[4,16,128]{2,1,0:T(8,128)S(1)}, u32[]{:S(2)}, u32[]{:S(2)}) collective-permute-start(f32[4,16,128]{2,1,0:T(8,128)S(1)} %get-tuple-element.46), channel_id=1, source_target_pairs={{0,30},{2,4},{4,2},{6,8},{8,6},{10,12},{12,10},{14,16},{16,14},{18... | collective-permute-start | bytes 98312 | tf_op jit(solution)/shard_map/ppermute | solution.py:574
  18.4 0.0 collective-permute-done.4.near_ref
  18.4 3.7 %collective-permute-done.5.far_ref = f32[4,16,128]{2,1,0:T(8,128)S(1)} collective-permute-done((f32[4,16,128]{2,1,0:T(8,128)S(1)}, f32[4,16,128]{2,1,0:T(8,128)S(1)}, u32[]{:S(2)}, u32[]{:S(2)}) %collective-permute-start.5) | collective-permute-done | bytes 32800 | tf_op jit(solution)/shard_map/ppermute | solution.py:574
  22.1 0.2 shard_map.91
  22.3 0.0 collective-permute-start.6
  22.3 0.7 %shard_map.92 = (f32[4,16,512]{2,1,0:T(8,128)S(1)}, f32[16,64]{1,0:T(8,128)S(1)}, f32[1,128]{1,0:T(1,128)S(1)}) custom-call(f32[4,16,512]{2,1,0:T(8,128)S(1)} %get-tuple-element.47.direction_ref.image_ref, bf16[4,512,512]{2,1,0:T(8,128)(2,1)S(1)} %get-tuple-element.38.flex_ref, f32[16,8,128]{2,1,0:T(8,128)S(1)} %get-tuple-element.35.weight_ref, ...), custom_call_target="tpu_custom_call" | custom-call | flops 100000000 | bytes 3000000 | tf_op jit(solution)/shard_map/pallas_call | solution.py:534
  23.0 0.5 %collective-permute-done.6.other_ref = f32[16,64]{1,0:T(8,128)S(1)} collective-permute-done((f32[16,64]{1,0:T(8,128)S(1)}, f32[16,64]{1,0:T(8,128)S(1)}, u32[]{:S(2)}, u32[]{:S(2)}) %collective-permute-start.6) | collective-permute-done | bytes 4128 | tf_op jit(solution)/shard_map/ppermute | solution.py:580
  23.5 0.4 shard_map.93
  23.9 3.9 %collective-permute-start.7 = (f32[4,16,128]{2,1,0:T(8,128)S(1)}, f32[4,16,128]{2,1,0:T(8,128)S(1)}, u32[]{:S(2)}, u32[]{:S(2)}) collective-permute-start(f32[4,16,128]{2,1,0:T(8,128)S(1)} %get-tuple-element.55), channel_id=1, source_target_pairs={{0,30},{2,0},{4,2},{6,4},{8,6},{10,8},{12,10},{14,12},{16,14},{18,... | collective-permute-start | bytes 98312 | tf_op jit(solution)/shard_map/ppermute | solution.py:571
  27.7 0.0 collective-permute-start.8
  27.7 13.0 %all_to_all.5 = f32[32,1,128]{2,1,0:T(1,128)S(1)} all-to-all(f32[32,1,128]{2,1,0:T(1,128)S(1)} %get-tuple-element.53), channel_id=1, replica_groups=mesh['district'=16,'coarse'=2] {'district','coarse'}, dimensions={0} | all-to-all | bytes 32768 | tf_op jit(solution)/shard_map/all_to_all | solution.py:681
  40.7 0.0 collective-permute-done.7.right_ref
  40.7 0.2 shard_map.94
  40.9 0.0 collective-permute-done.8.left_ref
  40.9 0.8 %shard_map.95 = (f32[4,16,512]{2,1,0:T(8,128)}, f32[4,16,512]{2,1,0:T(8,128)}) custom-call(f32[4,16,512]{2,1,0:T(8,128)S(1)} %get-tuple-element.56.multiplier_ref, f32[4,16,512]{2,1,0:T(8,128)S(1)} %get-tuple-element.57.partial_ref, f32[8,128]{1,0:T(8,128)S(1)} %get-tuple-element.58.factor_ref, f32[4,16,128]{2,1,0:T(8,128)S(1)} %collective-permute-done.8.left_ref, ...), custom_call_target="tpu_custom_call" | custom-call | tf_op jit(solution)/shard_map/pallas_call | solution.py:534
Async XLA Ops:
  1.5 11.3 %collective-permute-start = (f32[4,16,128]{2,1,0:T(8,128)S(1)}, f32[4,16,128]{2,1,0:T(8,128)S(1)}, u32[]{:S(2)}, u32[]{:S(2)}) collective-permute-start(f32[4,16,128]{2,1,0:T(8,128)S(1)} %get-tuple-element.32), channel_id=1, source_target_pairs={{0,2},{2,0},{4,6},{6,4},{8,10},{10,8},{12,14},{14,12},{16,18},{18,... | collective-permute-start | bytes 98312 | tf_op jit(solution)/shard_map/ppermute | solution.py:575
  4.5 8.2 %collective-permute-start.1 = (f32[4,16,128]{2,1,0:T(8,128)S(1)}, f32[4,16,128]{2,1,0:T(8,128)S(1)}, u32[]{:S(2)}, u32[]{:S(2)}) collective-permute-start(f32[4,16,128]{2,1,0:T(8,128)S(1)} %get-tuple-element.33), channel_id=1, source_target_pairs={{0,30},{2,4},{4,2},{6,8},{8,6},{10,12},{12,10},{14,16},{16,14},{18... | collective-permute-start | bytes 98312 | tf_op jit(solution)/shard_map/ppermute | solution.py:574
  9.1 1.4 %collective-permute-start.2 = (s32[4,8]{1,0:T(4,128)}, s32[4,8]{1,0:T(4,128)S(1)}, u32[]{:S(2)}, u32[]{:S(2)}) collective-permute-start(s32[4,8]{1,0:T(4,128)} %owner_hbm.1), channel_id=1, source_target_pairs={{0,1},{1,0},{2,3},{3,2},{4,5},{5,4},{6,7},{7,6},{8,9},{9,8},{10,11... | collective-permute-start | bytes 392 | tf_op jit(solution)/shard_map/ppermute | solution.py:597
  13.0 1.2 %collective-permute-start.3 = (f32[16,64]{1,0:T(8,128)S(1)}, f32[16,64]{1,0:T(8,128)S(1)}, u32[]{:S(2)}, u32[]{:S(2)}) collective-permute-start(f32[16,64]{1,0:T(8,128)S(1)} %get-tuple-element.42.own_ref), channel_id=1, source_target_pairs={{0,1},{1,0},{2,3},{3,2},{4,5},{5,4},{6,7},{7,6},{8,9},{9,8},{10,11... | collective-permute-start | bytes 12296 | tf_op jit(solution)/shard_map/ppermute | solution.py:580
  14.4 4.0 %collective-permute-start.4 = (f32[4,16,128]{2,1,0:T(8,128)S(1)}, f32[4,16,128]{2,1,0:T(8,128)S(1)}, u32[]{:S(2)}, u32[]{:S(2)}) collective-permute-start(f32[4,16,128]{2,1,0:T(8,128)S(1)} %get-tuple-element.45), channel_id=1, source_target_pairs={{0,2},{2,0},{4,6},{6,4},{8,10},{10,8},{12,14},{14,12},{16,18},{18,... | collective-permute-start | bytes 98312 | tf_op jit(solution)/shard_map/ppermute | solution.py:575
  14.5 7.6 %collective-permute-start.5 = (f32[4,16,128]{2,1,0:T(8,128)S(1)}, f32[4,16,128]{2,1,0:T(8,128)S(1)}, u32[]{:S(2)}, u32[]{:S(2)}) collective-permute-start(f32[4,16,128]{2,1,0:T(8,128)S(1)} %get-tuple-element.46), channel_id=1, source_target_pairs={{0,30},{2,4},{4,2},{6,8},{8,6},{10,12},{12,10},{14,16},{16,14},{18... | collective-permute-start | bytes 98312 | tf_op jit(solution)/shard_map/ppermute | solution.py:574
  22.3 1.2 %collective-permute-start.6 = (f32[16,64]{1,0:T(8,128)S(1)}, f32[16,64]{1,0:T(8,128)S(1)}, u32[]{:S(2)}, u32[]{:S(2)}) collective-permute-start(f32[16,64]{1,0:T(8,128)S(1)} %get-tuple-element.49.own_ref), channel_id=1, source_target_pairs={{0,1},{1,0},{2,3},{3,2},{4,5},{5,4},{6,7},{7,6},{8,9},{9,8},{10,11... | collective-permute-start | bytes 12296 | tf_op jit(solution)/shard_map/ppermute | solution.py:580
  23.9 16.8 %collective-permute-start.7 = (f32[4,16,128]{2,1,0:T(8,128)S(1)}, f32[4,16,128]{2,1,0:T(8,128)S(1)}, u32[]{:S(2)}, u32[]{:S(2)}) collective-permute-start(f32[4,16,128]{2,1,0:T(8,128)S(1)} %get-tuple-element.55), channel_id=1, source_target_pairs={{0,30},{2,0},{4,2},{6,4},{8,6},{10,8},{12,10},{14,12},{16,14},{18,... | collective-permute-start | bytes 98312 | tf_op jit(solution)/shard_map/ppermute | solution.py:571
  27.7 13.2 %collective-permute-start.8 = (f32[4,16,128]{2,1,0:T(8,128)S(1)}, f32[4,16,128]{2,1,0:T(8,128)S(1)}, u32[]{:S(2)}, u32[]{:S(2)}) collective-permute-start(f32[4,16,128]{2,1,0:T(8,128)S(1)} %get-tuple-element.59), channel_id=1, source_target_pairs={{0,2},{2,4},{4,6},{6,8},{8,10},{10,12},{12,14},{14,16},{16,18},{18... | collective-permute-start | bytes 98312 | tf_op jit(solution)/shard_map/ppermute | solution.py:571
